TPU v7x, 768 devices: a whole 4x8x12 slice. The times are simulated.
768 devices in a mesh: ctx: 24 (over z, core), tp: 4 (over x), pp: 8 (over y).
Axes of the slice: x: 4, y: 8, z: 12, core: 2. Of those that a mesh axis runs over, the one named last changes fastest.
Arguments:
- queries: bfloat16 [8, 3072, 4096], P('pp', 'ctx', 'tp'), may hold values from -0.59765625 to 0.59765625
- key_input: bfloat16 [8, 3072, 4096], P('pp', 'ctx', 'tp'), may hold values from -6 to 6
- values: bfloat16 [8, 3072, 4096], P('pp', 'ctx', 'tp'), may hold values from -6 to 6
- log_decay: float32 [8, 3072, 32], P('pp', 'ctx', 'tp'), may hold values from -1 to 0
- conv_weight: float32 [8, 4, 4096], P('pp', None, 'tp'), may hold values from -3 to 3
- out_grad: bfloat16 [8, 3072, 4096], P('pp', 'ctx', 'tp'), may hold values from -6 to 6
Outputs:
- layer_output: bfloat16 [8, 3072, 4096], P('pp', 'ctx', 'tp')
- input_grad_next: bfloat16 [8, 3072, 4096], P('pp', 'ctx', 'tp')
All inputs are finite; a program needn't handle non-finite values.
Results may differ from a plain program's by a relative error of at most 0.006.
The roundings to bfloat16 on the way count: a program that leaves them out, or rounds other values in their place, can miss the bound.
Values may be sent and summed in bfloat16 or wider, within the bound.
A program may use at most 32 MiB of HBM per device.

v0:
```python
import jax
import jax.numpy as jnp
from jax import lax
from jax.sharding import PartitionSpec as P


def shifted(block, axis, distance):
    devices = range(lax.axis_size(axis))
    route = [(i - distance, i) for i in devices if i - distance in devices]
    return lax.ppermute(block, axis, route)


def entering(value, axis, combine, identity):
    peers, place = (lax.axis_size(axis), lax.axis_index(axis))
    everything = jax.tree.map(lambda part: lax.all_gather(part, axis), value)
    start = jax.tree.map(
        lambda part, zero: jnp.broadcast_to(jnp.asarray(zero, part.dtype), part.shape),
        value,
        identity,
    )

    def step(k, before):
        reached = k < place
        new = combine(before, jax.tree.map(lambda part: part[k], everything))
        return jax.tree.map(lambda a, b: jnp.where(reached, a, b), new, before)

    return lax.fori_loop(0, peers, step, start)


def carried_in(value, axis, join, neutral):
    count = lax.axis_size(axis)
    place = lax.axis_index(axis)
    ahead = count - 1 - place
    gathered = jax.tree.map(
        lambda a, kind: lax.all_gather(a.astype(kind), axis), value, (jnp.bfloat16, jnp.bfloat16)
    )
    state = jax.tree.map(lambda a, e: jnp.zeros_like(a) + jnp.asarray(e, a.dtype), value, neutral)

    def one(step, state):
        source = count - 1 - step
        return join(
            state,
            jax.tree.map(
                lambda a, own: lax.dynamic_index_in_dim(a, source, 0, False).astype(own.dtype),
                gathered,
                value,
            ),
        )

    return lax.fori_loop(0, ahead, one, state)


def combine(first_part, second_part):
    return (
        first_part[0] + second_part[0],
        jnp.exp(second_part[0])[:, None, None] * first_part[1] + second_part[1],
    )


def decay_table(cum_decay):
    transposed = jnp.swapaxes(cum_decay, 0, 1)
    differ = transposed[:, :, None] - transposed[:, None, :]
    tok_rows = cum_decay.shape[0]
    causal = jnp.arange(tok_rows)[:, None] >= jnp.arange(tok_rows)[None, :]
    return jnp.where(causal, jnp.exp(jnp.where(causal, differ, 0.0)), 0.0)


def per_device(queries, key_input, values, log_decay, conv_weight, out_grad):
    tok_rows = queries.shape[1]
    feat_width = queries.shape[2]
    heads_dev = log_decay.shape[2]
    head_dim = feat_width // heads_dev
    tap_count = conv_weight.shape[1]
    width_all = feat_width * lax.axis_size("tp")
    tap_weights = conv_weight[0]
    head_shape = (tok_rows, heads_dev, head_dim)
    edge_rows = shifted(key_input[0, tok_rows - (tap_count - 1) :], "ctx", 1)
    extended = jnp.concatenate([edge_rows, key_input[0]], 0).astype(jnp.float32)
    conv_sum = jnp.zeros((tok_rows, feat_width), jnp.float32)
    for tap_index in range(tap_count):
        start_row = tap_count - 1 - tap_index
        conv_sum = conv_sum + tap_weights[tap_index] * extended[start_row : start_row + tok_rows]
    smoothed_key_rows = conv_sum.astype(jnp.bfloat16).reshape(head_shape)
    query_tile_block = queries[0].reshape(head_shape)
    value_tile_block = values[0].reshape(head_shape)
    grad_blk = out_grad[0].reshape(head_shape).astype(jnp.float32)
    cum_decay = jnp.cumsum(log_decay[0], axis=0)
    block_total = cum_decay[-1]
    mixing = decay_table(cum_decay)
    scores = jnp.einsum(
        "thk,shk->hts", query_tile_block, smoothed_key_rows, preferred_element_type=jnp.float32
    )
    weights = (scores * mixing).astype(jnp.bfloat16)
    weight_after = jnp.exp(block_total[None, :] - cum_decay)[:, :, None]
    keys_times_decay = (smoothed_key_rows.astype(jnp.float32) * weight_after).astype(jnp.bfloat16)
    block_state = jnp.einsum(
        "pto,ptd->tod", keys_times_decay, value_tile_block, preferred_element_type=jnp.float32
    )
    identity = (
        jnp.zeros((heads_dev,), jnp.float32),
        jnp.zeros((heads_dev, head_dim, head_dim), jnp.float32),
    )
    _, leading_rows = entering((block_total, block_state), "ctx", combine, identity)
    opening_half = leading_rows.astype(jnp.bfloat16)
    growth = jnp.exp(cum_decay)[:, :, None]
    attended = jnp.einsum(
        "hts,shv->thv", weights, value_tile_block, preferred_element_type=jnp.float32
    )
    attended = attended + growth * jnp.einsum(
        "upg,pgn->upn", query_tile_block, opening_half, preferred_element_type=jnp.float32
    )
    squares_local = jnp.sum(attended * attended, axis=(1, 2))
    squares_all = lax.psum(squares_local, "tp")
    root_mean = jnp.sqrt(squares_all / width_all + 1e-06)
    normed = attended / root_mean[:, None, None]
    shift_mean = lax.psum(jnp.sum(grad_blk * normed, axis=(1, 2)), "tp") / width_all
    layer_output = normed.astype(jnp.bfloat16).reshape(1, tok_rows, feat_width)
    gradient_of_attended = (
        (grad_blk - normed * shift_mean[:, None, None]) / root_mean[:, None, None]
    ).astype(jnp.bfloat16)
    queries_times_decay = (query_tile_block.astype(jnp.float32) * growth).astype(jnp.bfloat16)
    block_adjoint = jnp.einsum(
        "ezr,ezs->zrs",
        queries_times_decay,
        gradient_of_attended,
        preferred_element_type=jnp.float32,
    )
    _, state_following = carried_in((block_total, block_adjoint), "ctx", combine, identity)
    trailing_half = state_following.astype(jnp.bfloat16)
    score_grad = (
        jnp.einsum(
            "thv,shv->hts",
            gradient_of_attended,
            value_tile_block,
            preferred_element_type=jnp.float32,
        )
        * mixing
    ).astype(jnp.bfloat16)
    query_grad = jnp.einsum(
        "hts,shk->thk", score_grad, smoothed_key_rows, preferred_element_type=jnp.float32
    )
    query_grad = query_grad + growth * jnp.einsum(
        "csp,sqp->csq", gradient_of_attended, opening_half, preferred_element_type=jnp.float32
    )
    value_grad = jnp.einsum(
        "hts,thv->shv", weights, gradient_of_attended, preferred_element_type=jnp.float32
    )
    value_grad = value_grad + weight_after * jnp.einsum(
        "gnf,nfb->gnb", smoothed_key_rows, trailing_half, preferred_element_type=jnp.float32
    )
    ckey_grad = jnp.einsum(
        "hts,thk->shk", score_grad, query_tile_block, preferred_element_type=jnp.float32
    )
    ckey_grad = ckey_grad + weight_after * jnp.einsum(
        "cmj,mnj->cmn", value_tile_block, trailing_half, preferred_element_type=jnp.float32
    )
    grad_flat = ckey_grad.reshape(tok_rows, feat_width)
    next_rows = shifted(grad_flat[: tap_count - 1], "ctx", -1)
    padded_grad = jnp.concatenate([grad_flat, next_rows], 0)
    input_grad = query_grad.reshape(tok_rows, feat_width) + value_grad.reshape(tok_rows, feat_width)
    for tap_index in range(tap_count):
        input_grad = (
            input_grad + tap_weights[tap_index] * padded_grad[tap_index : tap_index + tok_rows]
        )
    input_send = input_grad.astype(jnp.bfloat16).reshape(1, tok_rows, feat_width)
    input_next = shifted(input_send, "pp", -1)
    return (layer_output, input_next)


def solution(mesh):
    placed = (
        P("pp", "ctx", "tp"),
        P("pp", "ctx", "tp"),
        P("pp", "ctx", "tp"),
        P("pp", "ctx", "tp"),
        P("pp", None, "tp"),
        P("pp", "ctx", "tp"),
    )
    return jax.shard_map(
        per_device,
        mesh=mesh,
        in_specs=placed,
        out_specs=(P("pp", "ctx", "tp"), P("pp", "ctx", "tp")),
        check_vma=False,
    )
```

profile of v0, /device:TPU:27, one launch (start us, length us, event | category | flops | bytes accessed | tf_op | source)
XLA Modules:
  0.0 271.6 jit_solution(2106866497092869838)
XLA Ops:
  7.9 4.5 %collective-permute-start = (bf16[3,1024]{1,0:T(4,128)(2,1)S(1)}, bf16[3,1024]{1,0:T(4,128)(2,1)S(1)}, u32[]{:S(2)}, u32[]{:S(2)}) collective-permute-start(bf16[3,1024]{1,0:T(4,128)(2,1)S(1)} %slice_bitcast_fusion), channel_id=1, source_target_pairs={{0,32},{32,64},{64,96},{96,128},{128,160},{160,192},{192,224},{224... | collective-permute-start | bytes 18440 | tf_op jit(solution)/shard_map/ppermute | solution.py:10
  18.1 1.1 copy.77
  20.4 30.9 %all-gather.2 = f32[24,1,8]{2,1,0:T(1,128)S(1)} all-gather(f32[1,1,8]{2,1,0:T(1,128)S(1)} %get-tuple-element.246), channel_id=1, replica_groups=mesh['ctx'=24,'tp'=4,'pp'=8] {'ctx'}, dimensions={0}, use_global_device_ids=true | all-gather | bytes 800 | tf_op jit(solution)/shard_map/all_gather | solution.py:15
  51.9 57.0 %all-gather.7.cloned.1.call-done = f32[192,128,128]{2,1,0:T(8,128)} async-done(((f32[8,128,128]{2,1,0:T(8,128)}), f32[192,128,128]{2,1,0:T(8,128)}) %all-gather.7.cloned.1.call-update) | async-done | bytes 12582928 | tf_op jit(solution)/shard_map/all_gather | solution.py:15
  108.9 29.1 %while.29 = (s32[]{:T(128)}, f32[8,128,128]{2,1,0:T(8,128)S(1)}, s32[]{:T(128)}, f32[24,8]{1,0:T(8,128)S(1)}, f32[24,8,128,128]{3,2,1,0:T(8,128)}, /*index=5*/s32[]{:T(128)}, s32[]{:T(128)}) while((s32[]{:T(128)}, f32[8,128,128]{2,1,0:T(8,128)S(1)}, s32[]{:T(128)}, f32[24,8]{1,0:T(8,128)S(1)}, f32[24,8,128,128]{3,2,1,0:T(8,128)}, ...), condition=%wide.region_2.3_spmd.clone, body=%wide.region_1.2_spmd.clone.sunk | while | flops 524292 | bytes 1573065 | solution.py:27
  108.9 1.2 fusion.55
  110.2 1.2 fusion.55
  111.4 1.2 fusion.55
  112.6 1.2 fusion.55
  113.8 1.2 fusion.55
  115.0 1.2 fusion.55
  116.2 1.2 fusion.55
  117.5 1.2 fusion.55
  118.7 1.2 fusion.55
  119.9 1.2 fusion.55
  121.1 1.2 fusion.55
  122.3 1.2 fusion.55
  123.5 1.2 fusion.55
  124.7 1.2 fusion.55
  126.0 1.2 fusion.55
  127.2 1.2 fusion.55
  128.4 1.2 fusion.55
  129.6 1.2 fusion.55
  130.8 1.2 fusion.55
  132.0 1.2 fusion.55
  133.3 1.2 fusion.55
  134.5 1.2 fusion.55
  135.7 1.2 fusion.55
  136.9 1.2 fusion.55
  138.4 6.6 %psum.14 = f32[128]{0:T(128)S(1)} all-reduce(f32[128]{0:T(128)S(1)} %get-tuple-element.251), channel_id=1, replica_groups=mesh['ctx'=24,'tp'=4,'pp'=8] {'tp'}, use_global_device_ids=true, to_apply=%region_4.5 | all-reduce | flops 128 | bytes 1024 | tf_op jit(solution)/shard_map/psum | solution.py:113
  145.2 8.1 %psum.15 = f32[128]{0:T(128)S(1)} all-reduce(f32[128]{0:T(128)S(1)} %multiply_reduce_fusion), channel_id=1, replica_groups=mesh['ctx'=24,'tp'=4,'pp'=8] {'tp'}, use_global_device_ids=true, to_apply=%region_6.7 | all-reduce | flops 128 | bytes 1024 | tf_op jit(solution)/shard_map/psum | solution.py:116
  154.5 25.7 %all-gather.3 = bf16[24,1,8]{2,1,0:T(2,128)(2,1)S(1)} all-gather(bf16[1,1,8]{2,1,0:T(2,128)(2,1)S(1)} %convert_bitcast_fusion), channel_id=1, replica_groups=mesh['ctx'=24,'tp'=4,'pp'=8] {'ctx'}, dimensions={0}, use_global_device_ids=true | all-gather | bytes 400 | tf_op jit(solution)/shard_map/all_gather | solution.py:35
  180.6 40.0 %all-gather.9.cloned.1.call-done = bf16[192,128,128]{2,1,0:T(8,128)(2,1)} async-done(((bf16[8,128,128]{2,1,0:T(8,128)(2,1)}), bf16[192,128,128]{2,1,0:T(8,128)(2,1)}) %all-gather.9.cloned.1.call-update) | async-done | bytes 6291472 | tf_op jit(solution)/shard_map/all_gather | solution.py:35
  220.7 25.5 %while.28 = (s32[]{:T(128)}, f32[8,128,128]{2,1,0:T(8,128)S(1)}, s32[]{:T(128)}, bf16[24,8]{1,0:T(8,128)(2,1)S(1)}, bf16[24,8,128,128]{3,2,1,0:T(8,128)(2,1)}, /*index=5*/s32[]{:T(128)}, s32[]{:T(128)}, s32[]{:T(128)}, s32[]{:T(128)}) while((s32[]{:T(128)}, f32[8,128,128]{2,1,0:T(8,128)S(1)}, s32[]{:T(128)}, bf16[24,8]{1,0:T(8,128)(2,1)S(1)}, ...), condition=%wide.region_8.9_spmd, body=%wide.region_7.8_spmd.sunk | while | flops 393230 | bytes 1310947 | solution.py:50
  220.7 1.1 convert_add_fusion.2
  221.9 1.1 convert_add_fusion.2
  223.1 1.1 convert_add_fusion.2
  224.2 1.1 convert_add_fusion.2
  228.8 1.1 convert_add_fusion.2
  230.0 1.1 convert_add_fusion.2
  231.2 1.1 convert_add_fusion.2
  232.3 1.1 convert_add_fusion.2
  233.5 1.1 convert_add_fusion.2
  234.6 1.1 convert_add_fusion.2
  239.3 1.1 convert_add_fusion.2
  247.6 3.3 %collective-permute-start.1 = (f32[3,1024]{1,0:T(4,128)S(1)}, f32[3,1024]{1,0:T(4,128)S(1)}, u32[]{:S(2)}, u32[]{:S(2)}) collective-permute-start(f32[3,1024]{1,0:T(4,128)S(1)} %copy.108), channel_id=1, source_target_pairs={{32,0},{64,32},{96,64},{128,96},{160,128},{192,160},{224,192},{256... | collective-permute-start | bytes 36872 | tf_op jit(solution)/shard_map/ppermute | solution.py:10
  252.9 2.2 collective-permute-start.2
  255.9 8.2 %collective-permute-done.2 = bf16[1,128,1024]{2,1,0:T(8,128)(2,1)S(1)} collective-permute-done((bf16[1,128,1024]{2,1,0:T(8,128)(2,1)S(1)}, bf16[1,128,1024]{2,1,0:T(8,128)(2,1)S(1)}, u32[]{:S(2)}, u32[]{:S(2)}) %collective-permute-start.2) | collective-permute-done | bytes 262176 | tf_op jit(solution)/shard_map/ppermute | solution.py:10
  (108 shorter events, 27.9 us)
Async XLA Ops:
  7.2 101.8 %all-gather.7.cloned.1.call-start = ((), (), s32[]{:S(2)}) async-start(), calls=%async_computation | async-start | bytes 13107200 | tf_op jit(solution)/shard_map/all_gather | solution.py:15
  7.9 7.5 %collective-permute-start = (bf16[3,1024]{1,0:T(4,128)(2,1)S(1)}, bf16[3,1024]{1,0:T(4,128)(2,1)S(1)}, u32[]{:S(2)}, u32[]{:S(2)}) collective-permute-start(bf16[3,1024]{1,0:T(4,128)(2,1)S(1)} %slice_bitcast_fusion), channel_id=1, source_target_pairs={{0,32},{32,64},{64,96},{96,128},{128,160},{160,192},{192,224},{224... | collective-permute-start | bytes 18440 | tf_op jit(solution)/shard_map/ppermute | solution.py:10
  18.0 202.7 %all-gather.9.cloned.1.call-start = ((), (), s32[]{:S(2)}) async-start(), calls=%async_computation.1 | async-start | bytes 6553600 | tf_op jit(solution)/shard_map/all_gather | solution.py:35
  51.6 101.7 %copy-start = (bf16[8,128,128]{1,2,0:T(8,128)(2,1)}, bf16[8,128,128]{1,2,0:T(8,128)(2,1)S(1)}, u32[]{:S(2)}) copy-start(bf16[8,128,128]{1,2,0:T(8,128)(2,1)S(1)} %fusion.12) | copy-start | bytes 786436
  153.3 93.5 %copy-start.1 = (bf16[8,128,128]{1,2,0:T(8,128)(2,1)S(1)}, bf16[8,128,128]{1,2,0:T(8,128)(2,1)}, u32[]{:S(2)}) copy-start(bf16[8,128,128]{1,2,0:T(8,128)(2,1)} %copy-done) | copy-start | bytes 786436
  247.6 5.1 %collective-permute-start.1 = (f32[3,1024]{1,0:T(4,128)S(1)}, f32[3,1024]{1,0:T(4,128)S(1)}, u32[]{:S(2)}, u32[]{:S(2)}) collective-permute-start(f32[3,1024]{1,0:T(4,128)S(1)} %copy.108), channel_id=1, source_target_pairs={{32,0},{64,32},{96,64},{128,96},{160,128},{192,160},{224,192},{256... | collective-permute-start | bytes 36872 | tf_op jit(solution)/shard_map/ppermute | solution.py:10
  252.9 11.2 %collective-permute-start.2 = (bf16[1,128,1024]{2,1,0:T(8,128)(2,1)S(1)}, bf16[1,128,1024]{2,1,0:T(8,128)(2,1)S(1)}, u32[]{:S(2)}, u32[]{:S(2)}) collective-permute-start(bf16[1,128,1024]{2,1,0:T(8,128)(2,1)S(1)} %fusion.29), channel_id=1, source_target_pairs={{1,0},{2,1},{3,2},{4,3},{5,4},{6,5},{7,6},{9,8},{10,9},{11,10},{12... | collective-permute-start | bytes 786440 | tf_op jit(solution)/shard_map/ppermute | solution.py:10
Sparse Core Ops, SparseCore 0:
  18.1 90.7 all-gather.6
  154.6 66.0 all-gather.8
where the time goes:
time: 274 us; the launch traced here: 272 us
  waiting for transfers between devices  106 us (39%)
  blocking collectives  71.2 us (26%)
  other arithmetic  54.9 us (20%)
  between operations  14.3 us (5%)
  starting transfers between devices  10.1 us (4%)
  local copies, waits for them, and re-layouts  8.44 us (3%)
  matrix products  4.86 us (2%)
    all_gather x1, waiting for transfers between devices, entering(): everything = jax.tree.map(lambda part: lax.all_gather(part, axis), value)  57 us
    all_gather x1, waiting for transfers between devices, carried_in(): lax.all_gather(a.astype(kind), axis)  40 us
    all_gather x1, blocking collectives, entering(): everything = jax.tree.map(lambda part: lax.all_gather(part, axis), value)  30.9 us
    select_n x24, other arithmetic, step(): return jax.tree.map(lambda a, b: jnp.where(reached, a, b), new, before)  28.1 us
    all_gather x1, blocking collectives, carried_in(): lax.all_gather(a.astype(kind), axis)  25.7 us
    add x22, other arithmetic, combine(): jnp.exp(second_part[0])[:, None, None] * first_part[1] + second_part[1]  24.4 us
    ppermute x3, starting transfers between devices, shifted(): return lax.ppermute(block, axis, route)  10 us
    ppermute x3, waiting for transfers between devices, shifted(): return lax.ppermute(block, axis, route)  9.28 us
  transfers between devices with their start and end apart: 5, of which 4 were waited for; matrix products, arithmetic and copies ran while one was open for 3% of the time, Pallas kernels for 0%

commit v1 on v0

v1 whole, which is shorter than its diff:
```python
import jax
import jax.numpy as jnp
from jax import lax
from jax.experimental import pallas as pl
from jax.experimental.pallas import tpu as pltpu
from jax.sharding import PartitionSpec as P

MESH = pl.DeviceIdType.MESH
F32 = jnp.float32
BF16 = jnp.bfloat16
HALO = 8
CHUNK = 32
GROUP = 2


def remote(src, dst, send_sem, recv_sem, where):
    return pltpu.make_async_remote_copy(
        src_ref=src,
        dst_ref=dst,
        send_sem=send_sem,
        recv_sem=recv_sem,
        device_id=where,
        device_id_type=MESH,
    )


def dot(a, b, dims):
    return lax.dot_general(a, b, (dims, ((), ())), preferred_element_type=F32)


NN = ((1,), (0,))
NT = ((1,), (1,))
TN = ((0,), (0,))


def kernel(
    ctx_n, tp_n, pp_n,
    q_hbm, k_hbm, v_hbm, ld_ref, w_ref, og_hbm,
    out_ref, gin_ref,
    q_ref, k_ref, v_ref, og_ref, halo_ref, kext, kc, grow, after, mix, wts, att, ag, acc, ckg, gst,
    cdt, bt, bt_p, acc_sq, acc_dot, tpbuf,
    s_m, s_t, f_in, f_out, p_half, p_stage,
    b_m, b_t, r_in, r_out, a_half, a_stage,
    load_sem, halo_s, halo_r, bt_s, bt_r, sx_s, sx_r, fc_s, fc_r, px_s, px_r,
    tp_s, tp_r, bx_s, bx_r, rc_s, rc_r, ax_s, ax_r, ch_s, ch_r, pp_s, pp_r,
):
    toks, feats = q_hbm.shape
    heads = ld_ref.shape[1]
    hd = feats // heads
    half = heads // 2
    taps = w_ref.shape[0]
    chunks = hd // CHUNK
    width_all = feats * tp_n
    ctx = lax.axis_index("ctx")
    tp = lax.axis_index("tp")
    pp = lax.axis_index("pp")
    core = lax.rem(ctx, 2)
    partner = ctx + 1 - 2 * core
    own0 = half * core
    their0 = half * (1 - core)
    z_first = ctx < 2
    z_last = ctx >= ctx_n - 2

    def lanes(h):
        return pl.ds(pl.multiple_of(h * hd, hd), hd)

    barrier = pltpu.get_barrier_semaphore()
    greet = []
    for step in (1, ctx_n - 1, 2, ctx_n - 2):
        greet.append({"ctx": lax.rem(ctx + step, ctx_n)})
    for step in range(1, tp_n):
        greet.append({"tp": lax.rem(tp + step, tp_n)})
    for step in (1, pp_n - 1):
        greet.append({"pp": lax.rem(pp + step, pp_n)})
    for where in greet:
        pl.semaphore_signal(barrier, inc=1, device_id=where, device_id_type=MESH)

    loads = [
        pltpu.make_async_copy(src, dst, load_sem.at[n])
        for n, (src, dst) in enumerate(
            ((k_hbm, k_ref), (v_hbm, v_ref), (q_hbm, q_ref), (og_hbm, og_ref))
        )
    ]
    for load in loads:
        load.start()

    rows_i = lax.broadcasted_iota(jnp.int32, (toks, toks), 0)
    cols_i = lax.broadcasted_iota(jnp.int32, (toks, toks), 1)
    causal = rows_i >= cols_i
    tri = causal.astype(F32)
    ld = ld_ref[...]
    cd = lax.dot_general(
        tri, ld, (NN, ((), ())), precision=lax.Precision.HIGHEST, preferred_element_type=F32
    )
    cdt[...] = lax.dot_general(
        ld, tri, (((0,), (1,)), ((), ())), precision=lax.Precision.HIGHEST,
        preferred_element_type=F32,
    )
    for h in range(heads):
        wide = jnp.broadcast_to(cd[:, h : h + 1], (toks, hd))
        total = wide[toks - 1 : toks, :]
        bt[h : h + 1, :] = total
        grow[:, h * hd : (h + 1) * hd] = jnp.exp(wide)
        after[:, h * hd : (h + 1) * hd] = jnp.exp(total - wide)
        differ = wide - cdt[h : h + 1, :]
        mix[h] = jnp.where(causal, jnp.exp(jnp.where(causal, differ, 0.0)), 0.0)

    pl.semaphore_wait(barrier, len(greet))

    tail = halo_ref.shape[0]
    halo = remote(
        k_hbm.at[pl.ds(toks - tail, tail), :], halo_ref, halo_s, halo_r,
        {"ctx": lax.rem(ctx + 1, ctx_n)},
    )

    @pl.when(ctx < ctx_n - 1)
    def _():
        halo.start()

    @pl.when(ctx == 0)
    def _():
        halo_ref[...] = jnp.zeros_like(halo_ref)

    swap_bt = remote(bt, bt_p, bt_s, bt_r, {"ctx": partner})
    swap_bt.start()

    @pl.when(z_first)
    def _():
        f_in[...] = jnp.zeros_like(f_in)

    @pl.when(z_last)
    def _():
        r_in[...] = jnp.zeros_like(r_in)

    @pl.when(ctx == ctx_n - 1)
    def _():
        ckg[pl.ds(toks, HALO), :] = jnp.zeros((HALO, feats), F32)

    @pl.when(pp == pp_n - 1)
    def _():
        gin_ref[...] = jnp.zeros_like(gin_ref)

    loads[0].wait()
    kext[pl.ds(HALO, toks), :] = k_ref[...].astype(F32)
    loads[1].wait()

    @pl.when(ctx > 0)
    def _():
        halo.wait_recv()

    kext[pl.ds(0, HALO), :] = halo_ref[pl.ds(tail - HALO, HALO), :].astype(F32)

    def swap(mine, theirs, send_sem, recv_sem, i):
        return remote(
            mine.at[their0 + i], theirs.at[i], send_sem.at[i], recv_sem.at[i], {"ctx": partner}
        )

    def states(g, _):
        for j in range(GROUP):
            idx = g * GROUP + j
            h = lax.rem(their0 + idx, heads)
            hs = lanes(h)
            conv = w_ref[pl.ds(0, 1), hs] * kext[pl.ds(HALO, toks), hs]
            for tap in range(1, taps):
                conv = conv + w_ref[pl.ds(tap, 1), hs] * kext[pl.ds(HALO - tap, toks), hs]
            keys = conv.astype(BF16)
            kc[:, hs] = keys
            scaled = (keys.astype(F32) * after[:, hs]).astype(BF16)
            s_m[h] = dot(scaled, v_ref[:, hs], TN)

        @pl.when(g < half // GROUP)
        def _():
            for j in range(GROUP):
                swap(s_m, s_t, sx_s, sx_r, g * GROUP + j).start()

        return 0

    lax.fori_loop(0, heads // GROUP, states, 0)
    swap_bt.wait_recv()

    def forward_hop(n, i, c):
        piece = pl.ds(c * CHUNK, CHUNK)
        return remote(
            f_out.at[i, piece], f_in.at[i, piece], fc_s.at[n], fc_r.at[n],
            {"ctx": lax.rem(ctx + 2, ctx_n)},
        )

    def backward_hop(n, i, c):
        piece = pl.ds(c * CHUNK, CHUNK)
        return remote(
            r_out.at[i, piece], r_in.at[i, piece], rc_s.at[n], rc_r.at[n],
            {"ctx": lax.rem(ctx + ctx_n - 2, ctx_n)},
        )

    def hand(stage, dest, send_sem, recv_sem, i, h):
        return remote(
            stage.at[i], dest.at[h], send_sem.at[i], recv_sem.at[i], {"ctx": partner}
        )

    def relay(lead, first, last, hop, mine, theirs, into, out, dest, stage, xs, xr, hs_, hr_):
        lf = lead.astype(F32)

        def one(i, _):
            h = own0 + i
            e_m = jnp.exp(bt[pl.ds(h, 1), :])
            e_t = jnp.exp(bt_p[pl.ds(h, 1), :])
            both = e_m * e_t
            ca = lf * e_t + (1.0 - lf)
            cb = lf + (1.0 - lf) * e_m
            c1 = lf + (1.0 - lf) * e_t
            s1 = 1.0 - lf
            c2 = lf * e_m + (1.0 - lf)
            s2 = lf
            swap(mine, theirs, xs, xr, i).wait_recv()
            for c in range(chunks):
                piece = pl.ds(c * CHUNK, CHUNK)
                copy = hop(i * chunks + c, i, c)

                @pl.when(jnp.logical_not(first))
                def _():
                    copy.wait_recv()

                carry = into[i, piece, :]
                sm = mine[h, piece, :]
                st = theirs[i, piece, :]
                out[i, piece, :] = both * carry + (ca * sm + cb * st)

                @pl.when(jnp.logical_not(last))
                def _():
                    copy.start()

                stage[i, piece, :] = (c2 * carry + s2 * sm).astype(BF16)
                dest[h, piece, :] = (c1 * carry + s1 * st).astype(BF16)
            hand(stage, dest, hs_, hr_, i, h).start()
            return 0

        lax.fori_loop(0, half, one, 0)

    def forward_relay():
        relay(
            core == 0, z_first, z_last, forward_hop, s_m, s_t, f_in, f_out, p_half, p_stage,
            sx_s, sx_r, px_s, px_r,
        )

    early_f = ctx < 2 * max(1, ctx_n // 8)

    @pl.when(early_f)
    def _():
        forward_relay()

    loads[2].wait()

    def inside(g, _):
        for j in range(GROUP):
            h = g * GROUP + j
            hs = lanes(h)
            scores = dot(q_ref[:, hs], kc[:, hs], NT)
            w = (scores * mix[h]).astype(BF16)
            wts[h] = w
            att[:, hs] = dot(w, v_ref[:, hs], NN)
        return 0

    lax.fori_loop(0, heads // GROUP, inside, 0)

    @pl.when(jnp.logical_not(early_f))
    def _():
        forward_relay()

    loads[3].wait()
    acc_sq[...] = jnp.zeros_like(acc_sq)
    acc_dot[...] = jnp.zeros_like(acc_dot)

    def attend(g, _):
        @pl.when(g >= half // GROUP)
        def _():
            for j in range(GROUP):
                i = g * GROUP + j - half
                hand(p_stage, p_half, px_s, px_r, i, their0 + i).wait_recv()

        for j in range(GROUP):
            h = lax.rem(own0 + g * GROUP + j, heads)
            hs = lanes(h)
            a = att[:, hs] + grow[:, hs] * dot(q_ref[:, hs], p_half[h], NN)
            att[:, hs] = a
            acc_sq[...] += a * a
            acc_dot[...] += a * og_ref[:, hs].astype(F32)
        return 0

    lax.fori_loop(0, heads // GROUP, attend, 0)

    sq_row = jnp.sum(acc_sq[...].T, axis=0, keepdims=True)
    dot_row = jnp.sum(acc_dot[...].T, axis=0, keepdims=True)
    first_row = lax.broadcasted_iota(jnp.int32, (8, toks), 0) == 0
    tpbuf[0] = jnp.where(first_row, sq_row, dot_row)

    def sums(step):
        return remote(
            tpbuf.at[0], tpbuf.at[step], tp_s.at[step - 1], tp_r.at[step - 1],
            {"tp": lax.rem(tp + step, tp_n)},
        )

    for step in range(1, tp_n):
        sums(step).start()
    for step in range(1, tp_n):
        sums(step).wait_recv()
    sums_all = tpbuf[0]
    for step in range(1, tp_n):
        sums_all = sums_all + tpbuf[step]
    inv_row = 1.0 / jnp.sqrt(sums_all[0:1, :] / width_all + 1e-06)
    shift_row = (sums_all[1:2, :] / width_all) * inv_row
    inv = jnp.broadcast_to(inv_row, (hd, toks)).T
    shift = jnp.broadcast_to(shift_row, (hd, toks)).T

    def adjoints(g, _):
        for j in range(GROUP):
            idx = g * GROUP + j
            h = lax.rem(their0 + idx, heads)
            hs = lanes(h)
            normed = att[:, hs] * inv
            out_ref[:, hs] = normed.astype(BF16)
            grad = ((og_ref[:, hs].astype(F32) - normed * shift) * inv).astype(BF16)
            ag[:, hs] = grad
            sq = (q_ref[:, hs].astype(F32) * grow[:, hs]).astype(BF16)
            b_m[h] = dot(sq, grad, TN)

        @pl.when(g < half // GROUP)
        def _():
            for j in range(GROUP):
                swap(b_m, b_t, bx_s, bx_r, g * GROUP + j).start()

        return 0

    lax.fori_loop(0, heads // GROUP, adjoints, 0)

    def backward_relay():
        relay(
            core == 1, z_last, z_first, backward_hop, b_m, b_t, r_in, r_out, a_half, a_stage,
            bx_s, bx_r, ax_s, ax_r,
        )

    early_r = ctx >= ctx_n - 2 * max(1, ctx_n // 8)

    @pl.when(early_r)
    def _():
        backward_relay()

    def inside_grads(g, _):
        for j in range(GROUP):
            h = g * GROUP + j
            hs = lanes(h)
            grad = ag[:, hs]
            sg = (dot(grad, v_ref[:, hs], NT) * mix[h]).astype(BF16)
            qg = dot(sg, kc[:, hs], NN) + grow[:, hs] * dot(grad, p_half[h], NT)
            acc[:, hs] = qg + dot(wts[h], grad, TN)
            ckg[pl.ds(0, toks), hs] = dot(sg, q_ref[:, hs], TN)
        return 0

    lax.fori_loop(0, heads // GROUP, inside_grads, 0)

    @pl.when(jnp.logical_not(early_r))
    def _():
        backward_relay()

    def edge(h):
        hs = lanes(h)
        return remote(
            ckg.at[pl.ds(0, HALO), hs], ckg.at[pl.ds(toks, HALO), hs], ch_s.at[h], ch_r.at[h],
            {"ctx": lax.rem(ctx + ctx_n - 1, ctx_n)},
        )

    def outside_grads(g, _):
        @pl.when(g >= half // GROUP)
        def _():
            for j in range(GROUP):
                i = g * GROUP + j - half
                hand(a_stage, a_half, ax_s, ax_r, i, their0 + i).wait_recv()

        for j in range(GROUP):
            h = lax.rem(own0 + g * GROUP + j, heads)
            hs = lanes(h)
            wa = after[:, hs]
            state = a_half[h]
            ckg[pl.ds(0, toks), hs] += wa * dot(v_ref[:, hs], state, NT)
            acc[:, hs] += wa * dot(kc[:, hs], state, NN)

        @pl.when(ctx > 0)
        def _():
            for j in range(GROUP):
                edge(lax.rem(own0 + g * GROUP + j, heads)).start()

        return 0

    lax.fori_loop(0, heads // GROUP, outside_grads, 0)

    def back(h):
        hs = lanes(h)
        return remote(
            gst.at[:, hs], gin_ref.at[:, hs], pp_s.at[h], pp_r.at[h],
            {"pp": lax.rem(pp + pp_n - 1, pp_n)},
        )

    def finish(g, _):
        @pl.when(ctx < ctx_n - 1)
        def _():
            for j in range(GROUP):
                edge(lax.rem(own0 + g * GROUP + j, heads)).wait_recv()

        for j in range(GROUP):
            h = lax.rem(own0 + g * GROUP + j, heads)
            hs = lanes(h)
            total = acc[:, hs]
            for tap in range(taps):
                total = total + w_ref[pl.ds(tap, 1), hs] * ckg[pl.ds(tap, toks), hs]
            gst[:, hs] = total.astype(BF16)

        @pl.when(pp > 0)
        def _():
            for j in range(GROUP):
                back(lax.rem(own0 + g * GROUP + j, heads)).start()

        return 0

    lax.fori_loop(0, heads // GROUP, finish, 0)

    @pl.when(pp < pp_n - 1)
    def _():
        def arrive(h, _):
            back(h).wait_recv()
            return 0

        lax.fori_loop(0, heads, arrive, 0)

    @pl.when(pp > 0)
    def _():
        def leave(h, _):
            back(h).wait_send()
            return 0

        lax.fori_loop(0, heads, leave, 0)

    @pl.when(ctx < ctx_n - 1)
    def _():
        halo.wait_send()

    swap_bt.wait_send()
    for step in range(1, tp_n):
        sums(step).wait_send()

    @pl.when(ctx > 0)
    def _():
        def leave(h, _):
            edge(h).wait_send()
            return 0

        lax.fori_loop(0, heads, leave, 0)

    def leave(i, _):
        swap(s_m, s_t, sx_s, sx_r, i).wait_send()
        swap(b_m, b_t, bx_s, bx_r, i).wait_send()
        hand(p_stage, p_half, px_s, px_r, i, own0 + i).wait_send()
        hand(a_stage, a_half, ax_s, ax_r, i, own0 + i).wait_send()
        return 0

    lax.fori_loop(0, half, leave, 0)

    @pl.when(jnp.logical_not(z_last))
    def _():
        def leave(n, _):
            forward_hop(n, n // chunks, lax.rem(n, chunks)).wait_send()
            return 0

        lax.fori_loop(0, half * chunks, leave, 0)

    @pl.when(jnp.logical_not(z_first))
    def _():
        def leave(n, _):
            backward_hop(n, n // chunks, lax.rem(n, chunks)).wait_send()
            return 0

        lax.fori_loop(0, half * chunks, leave, 0)


def solution(mesh):
    ctx_n, tp_n, pp_n = mesh.shape["ctx"], mesh.shape["tp"], mesh.shape["pp"]

    def per_device(queries, key_input, values, log_decay, conv_weight, out_grad):
        toks, feats = queries.shape[1:]
        heads = log_decay.shape[2]
        hd = feats // heads
        half = heads // 2
        pieces = half * (hd // CHUNK)
        dma = pltpu.SemaphoreType.DMA
        flat_b = pltpu.VMEM((toks, feats), BF16)
        flat_f = pltpu.VMEM((toks, feats), F32)
        per_head_f = pltpu.VMEM((heads, hd, hd), F32)
        per_head_b = pltpu.VMEM((heads, hd, hd), BF16)
        half_f = pltpu.VMEM((half, hd, hd), F32)
        half_b = pltpu.VMEM((half, hd, hd), BF16)
        longer = pltpu.VMEM((toks + HALO, feats), F32)
        square = pltpu.VMEM((toks, hd), F32)
        rows = pltpu.VMEM((heads, hd), F32)
        scratch = [
            flat_b, flat_b, flat_b, flat_b, pltpu.VMEM((16, feats), BF16), longer, flat_b,
            flat_f, flat_f, pltpu.VMEM((heads, toks, toks), F32),
            pltpu.VMEM((heads, toks, toks), BF16), flat_f, flat_b, flat_f, longer, flat_b,
            pltpu.VMEM((heads, toks), F32), rows, rows, square, square,
            pltpu.VMEM((tp_n, 8, toks), F32),
            per_head_f, half_f, half_f, half_f, per_head_b, half_b,
            per_head_f, half_f, half_f, half_f, per_head_b, half_b,
            dma((4,)), dma, dma, dma, dma, dma((half,)), dma((half,)),
            dma((pieces,)), dma((pieces,)), dma((half,)), dma((half,)),
            dma((tp_n - 1,)), dma((tp_n - 1,)), dma((half,)), dma((half,)),
            dma((pieces,)), dma((pieces,)), dma((half,)), dma((half,)),
            dma((heads,)), dma((heads,)), dma((heads,)), dma((heads,)),
        ]
        whole = pl.BlockSpec(memory_space=pltpu.VMEM)
        there = pl.BlockSpec(memory_space=pl.ANY)

        def body(*refs):
            kernel(ctx_n, tp_n, pp_n, *refs)

        shape = jax.ShapeDtypeStruct((toks, feats), BF16)
        out, gin = pl.pallas_call(
            body,
            out_shape=(shape, shape),
            in_specs=[there, there, there, whole, whole, there],
            out_specs=(whole, whole),
            scratch_shapes=scratch,
            compiler_params=pltpu.CompilerParams(
                collective_id=0, has_side_effects=True, vmem_limit_bytes=40 * 1024 * 1024
            ),
        )(queries[0], key_input[0], values[0], log_decay[0], conv_weight[0], out_grad[0])
        return out[None], gin[None]

    placed = (
        P("pp", "ctx", "tp"),
        P("pp", "ctx", "tp"),
        P("pp", "ctx", "tp"),
        P("pp", "ctx", "tp"),
        P("pp", None, "tp"),
        P("pp", "ctx", "tp"),
    )
    return jax.shard_map(
        per_device,
        mesh=mesh,
        in_specs=placed,
        out_specs=(P("pp", "ctx", "tp"), P("pp", "ctx", "tp")),
        check_vma=False,
    )
```

time: 274 us -> 115 us (0.42)
  the two profiles are of different devices: /device:TPU:27 before, /device:TPU:25 now
where the time goes in v1:
time: 115 us
  Pallas kernels  107 us (93%)
  local copies, waits for them, and re-layouts  6.6 us (6%)
    pallas_call x1, Pallas kernels, per_device(): pl.pallas_call(body, out_shape=(shape, shape), in_specs=[there, there, th...  107 us
    unnamed x15, local copies, waits for them, and re-layouts  6.6 us

profile of v1, /device:TPU:25, one launch (start us, length us, event | category | flops | bytes accessed | tf_op | source)
XLA Modules:
  0.0 114.6 jit_solution(5319472402501231479)
XLA Ops:
  0.6 0.0 copy-start.5
  0.6 0.7 copy-done.5
  1.3 0.0 copy-start.4
  1.3 0.1 copy.8
  1.4 0.6 copy-done.4
  2.0 0.0 copy-start
  2.0 0.9 copy-done
  3.0 0.0 copy-start.1
  3.0 0.9 copy-done.1
  3.9 0.0 copy-start.2
  3.9 0.9 copy-done.2
  4.9 0.0 copy-start.3
  4.9 0.9 copy-done.3
  5.8 107.4 %shard_map.77 = (bf16[128,1024]{1,0:T(8,128)(2,1)S(1)}, bf16[128,1024]{1,0:T(8,128)(2,1)S(1)}) custom-call(bf16[128,1024]{1,0:T(8,128)(2,1)S(1)} %bitcast.8, bf16[128,1024]{1,0:T(8,128)(2,1)S(1)} %bitcast.9, bf16[128,1024]{1,0:T(8,128)(2,1)S(1)} %bitcast.10, f32[128,8]{1,0:T(8,128)S(1)} %bitcast.12, f32[4,1024]{1,0:T(4,128)S(1)} %bitcast.15, ...), custom_call_target="tpu_custom_call" | custom-call | tf_op jit(solution)/shard_map/pallas_call | solution.py:523
  113.2 0.7 copy.11
  113.9 0.7 copy.12
Async XLA Ops:
  0.6 0.7 copy-start.5
  1.3 0.7 copy-start.4
  2.0 0.9 copy-start
  3.0 0.9 copy-start.1
  3.9 0.9 copy-start.2
  4.9 0.9 copy-start.3

commit v2 on v1

v2 whole, which is shorter than its diff:
```python
import jax
import jax.numpy as jnp
from jax import lax
from jax.experimental import pallas as pl
from jax.experimental.pallas import tpu as pltpu
from jax.sharding import PartitionSpec as P

MESH = pl.DeviceIdType.MESH
F32 = jnp.float32
BF16 = jnp.bfloat16
HALO = 8
GROUP = 2


def remote(src, dst, send_sem, recv_sem, where):
    return pltpu.make_async_remote_copy(
        src_ref=src,
        dst_ref=dst,
        send_sem=send_sem,
        recv_sem=recv_sem,
        device_id=where,
        device_id_type=MESH,
    )


def dot(a, b, dims):
    return lax.dot_general(a, b, (dims, ((), ())), preferred_element_type=F32)


NN = ((1,), (0,))
NT = ((1,), (1,))
TN = ((0,), (0,))


def kernel(
    ctx_n, tp_n, pp_n,
    q_hbm, k_hbm, v_hbm, ld_ref, w_ref, og_hbm,
    out_ref, gin_ref,
    q_ref, k_ref, v_ref, og_ref, halo_ref, kext, kc, grow, after, mix, wts, att, ag, acc, ckg, gst,
    bt, bt_all, acc_sq, acc_dot, tpbuf,
    s_out, s_in, p_out, p_in, b_out, b_in, a_out, a_in,
    load_sem, halo_s, halo_r, bt_s, bt_r, tp_s, tp_r,
    s_s, s_r, p_s, p_r, b_s, b_r, a_s, a_r, ch_s, ch_r, pp_s, pp_r,
):
    toks, feats = q_hbm.shape
    heads = ld_ref.shape[0]
    hd = feats // heads
    taps = w_ref.shape[0]
    width_all = feats * tp_n
    parts = ctx_n // heads
    rows = s_in.shape[1]
    group = min(GROUP, heads)
    steps = heads // group
    ctx = lax.axis_index("ctx")
    tp = lax.axis_index("tp")
    pp = lax.axis_index("pp")
    my_head = ctx // parts
    my_part = lax.rem(ctx, parts)
    far_head = lax.rem(ctx + ctx_n // 2, ctx_n) // parts

    def lanes(h):
        return pl.ds(pl.multiple_of(h * hd, hd), hd)

    def begin(part):
        return part * rows - (part // (parts - 1)) * (parts * rows - hd)

    def fan(idx):
        return ((idx + 1) // 2) * (2 * lax.rem(idx, 2) - 1)

    def far_first(idx):
        return lax.rem(far_head + fan(idx) + heads, heads)

    def near_first(idx):
        return lax.rem(my_head + fan(idx) + heads, heads)

    barrier = pltpu.get_barrier_semaphore()
    greet = [{"ctx": lax.rem(ctx + step, ctx_n)} for step in range(1, ctx_n)]
    greet += [{"tp": lax.rem(tp + step, tp_n)} for step in range(1, tp_n)]
    if pp_n > 1:
        greet += [{"pp": lax.rem(pp + step, pp_n)} for step in (1, pp_n - 1)]
    for where in greet:
        pl.semaphore_signal(barrier, inc=1, device_id=where, device_id_type=MESH)

    loads = [
        pltpu.make_async_copy(src, dst, load_sem.at[n])
        for n, (src, dst) in enumerate(
            ((k_hbm, k_ref), (v_hbm, v_ref), (q_hbm, q_ref), (og_hbm, og_ref))
        )
    ]
    for load in loads:
        load.start()

    rows_i = lax.broadcasted_iota(jnp.int32, (toks, toks), 0)
    cols_i = lax.broadcasted_iota(jnp.int32, (toks, toks), 1)
    causal = rows_i >= cols_i
    tri = causal.astype(F32)
    ld = ld_ref[...]
    cd = lax.dot_general(
        tri, ld, (NT, ((), ())), precision=lax.Precision.HIGHEST, preferred_element_type=F32
    )
    cdt = lax.dot_general(
        ld, tri, (NT, ((), ())), precision=lax.Precision.HIGHEST, preferred_element_type=F32
    )
    for h in range(heads):
        wide = jnp.broadcast_to(cd[:, h : h + 1], (toks, hd))
        total = wide[toks - 1 : toks, :]
        bt[h] = total
        grow[:, h * hd : (h + 1) * hd] = jnp.exp(wide)
        after[:, h * hd : (h + 1) * hd] = jnp.exp(total - wide)
        differ = wide - cdt[h : h + 1, :]
        mix[h] = jnp.where(causal, jnp.exp(jnp.where(causal, differ, 0.0)), 0.0)

    pl.semaphore_wait(barrier, len(greet))

    tail = halo_ref.shape[0]
    halo = remote(
        k_hbm.at[pl.ds(toks - tail, tail), :], halo_ref, halo_s, halo_r,
        {"ctx": lax.rem(ctx + 1, ctx_n)},
    )

    @pl.when(ctx < ctx_n - 1)
    def _():
        halo.start()

    def total_to(step):
        peer = lax.rem(ctx + step, ctx_n)
        return remote(
            bt.at[peer // parts], bt_all.at[ctx], bt_s.at[step - 1], bt_r.at[step - 1],
            {"ctx": peer},
        )

    def send_total(step, _):
        total_to(step).start()
        return 0

    lax.fori_loop(1, ctx_n, send_total, 0)
    bt_all[ctx] = bt[my_head]

    @pl.when(ctx == 0)
    def _():
        halo_ref[...] = jnp.zeros_like(halo_ref)

    @pl.when(ctx == ctx_n - 1)
    def _():
        ckg[pl.ds(toks, HALO), :] = jnp.zeros((HALO, feats), F32)

    @pl.when(pp == pp_n - 1)
    def _():
        gin_ref[...] = jnp.zeros_like(gin_ref)

    loads[0].wait()
    kext[pl.ds(HALO, toks), :] = k_ref[...].astype(F32)
    loads[1].wait()

    @pl.when(ctx > 0)
    def _():
        halo.wait_recv()

    kext[pl.ds(0, HALO), :] = halo_ref[pl.ds(tail - HALO, HALO), :].astype(F32)

    def spread(src, dst, send_sem, recv_sem, h, part):
        owner = h * parts + part
        first = pl.multiple_of(begin(part), 16)
        return remote(
            src.at[h, pl.ds(first, rows)], dst.at[ctx], send_sem.at[owner], recv_sem.at[ctx],
            {"ctx": owner},
        )

    def spread_head(src, dst, send_sem, recv_sem, h):
        for part in range(parts):
            @pl.when(h * parts + part != ctx)
            def _():
                spread(src, dst, send_sem, recv_sem, h, part).start()

    def keep(src, dst):
        dst[ctx] = src[my_head, pl.ds(pl.multiple_of(begin(my_part), 16), rows), :]

    def deliver(src, dst, send_sem, recv_sem, c):
        return remote(
            src.at[c], dst.at[ctx], send_sem.at[c], recv_sem.at[ctx], {"ctx": c}
        )

    def arrive(src, recv_sem, n):
        return remote(src.at[n], src.at[n], recv_sem.at[n], recv_sem.at[n], {"ctx": ctx})

    def scan(into, recv_sem, out, home, send_sem, home_sem, order):
        def ready(step, _):
            n = lax.rem(ctx + step, ctx_n)
            arrive(into, recv_sem, n).wait_recv()
            return 0

        lax.fori_loop(1, ctx_n, ready, 0)
        carry = jnp.zeros((rows, hd), F32)
        for c in order:
            out[c] = carry.astype(BF16)
            carry = jnp.exp(bt_all[c]) * carry + into[c].astype(F32)

        def give(idx, _):
            c = lax.rem(ctx + ctx_n // 2 + fan(idx) + ctx_n, ctx_n)
            deliver(out, home, send_sem, home_sem, c).start()
            return 0

        lax.fori_loop(0, ctx_n - 1, give, 0)
        home[ctx] = out[ctx]

    def collect(home, home_sem, h):
        for part in range(parts):
            @pl.when(h * parts + part != ctx)
            def _():
                arrive(home, home_sem, h * parts + part).wait_recv()

    def whole(home, h):
        pieces = []
        for part in range(parts):
            piece = home[h * parts + part]
            pieces.append(piece[part * rows - begin(part) :, :])
        return jnp.concatenate(pieces, axis=0)

    def states(g, _):
        for j in range(group):
            h = far_first(g * group + j)
            hs = lanes(h)
            conv = w_ref[pl.ds(0, 1), hs] * kext[pl.ds(HALO, toks), hs]
            for tap in range(1, taps):
                conv = conv + w_ref[pl.ds(tap, 1), hs] * kext[pl.ds(HALO - tap, toks), hs]
            keys = conv.astype(BF16)
            kc[:, hs] = keys
            scaled = (keys.astype(F32) * after[:, hs]).astype(BF16)
            s_out[h] = dot(scaled, v_ref[:, hs], TN).astype(BF16)
        for j in range(group):
            spread_head(s_out, s_in, s_s, s_r, far_first(g * group + j))
        return 0

    lax.fori_loop(0, steps, states, 0)
    keep(s_out, s_in)
    loads[2].wait()

    def inside(g, _):
        for j in range(group):
            h = g * group + j
            hs = lanes(h)
            scores = dot(q_ref[:, hs], kc[:, hs], NT)
            w = (scores * mix[h]).astype(BF16)
            wts[h] = w
            att[:, hs] = dot(w, v_ref[:, hs], NN)
        return 0

    lax.fori_loop(0, steps, inside, 0)

    def total_in(step, _):
        total_to(step).wait_recv()
        return 0

    lax.fori_loop(1, ctx_n, total_in, 0)
    scan(s_in, s_r, p_out, p_in, p_s, p_r, range(ctx_n))

    loads[3].wait()
    acc_sq[...] = jnp.zeros_like(acc_sq)
    acc_dot[...] = jnp.zeros_like(acc_dot)

    def attend(g, _):
        for j in range(group):
            collect(p_in, p_r, near_first(g * group + j))
        for j in range(group):
            h = near_first(g * group + j)
            hs = lanes(h)
            a = att[:, hs] + grow[:, hs] * dot(q_ref[:, hs], whole(p_in, h), NN)
            att[:, hs] = a
            acc_sq[...] += a * a
            acc_dot[...] += a * og_ref[:, hs].astype(F32)
        return 0

    lax.fori_loop(0, steps, attend, 0)

    sq_row = jnp.sum(acc_sq[...].T, axis=0, keepdims=True)
    dot_row = jnp.sum(acc_dot[...].T, axis=0, keepdims=True)
    first_row = lax.broadcasted_iota(jnp.int32, (8, toks), 0) == 0
    tpbuf[0] = jnp.where(first_row, sq_row, dot_row)

    def sums(step):
        return remote(
            tpbuf.at[0], tpbuf.at[step], tp_s.at[step - 1], tp_r.at[step - 1],
            {"tp": lax.rem(tp + step, tp_n)},
        )

    for step in range(1, tp_n):
        sums(step).start()
    for step in range(1, tp_n):
        sums(step).wait_recv()
    sums_all = tpbuf[0]
    for step in range(1, tp_n):
        sums_all = sums_all + tpbuf[step]
    inv_row = 1.0 / jnp.sqrt(sums_all[0:1, :] / width_all + 1e-06)
    shift_row = (sums_all[1:2, :] / width_all) * inv_row
    inv = jnp.broadcast_to(inv_row, (hd, toks)).T
    shift = jnp.broadcast_to(shift_row, (hd, toks)).T

    def adjoints(g, _):
        for j in range(group):
            h = far_first(g * group + j)
            hs = lanes(h)
            normed = att[:, hs] * inv
            out_ref[:, hs] = normed.astype(BF16)
            grad = ((og_ref[:, hs].astype(F32) - normed * shift) * inv).astype(BF16)
            ag[:, hs] = grad
            sq = (q_ref[:, hs].astype(F32) * grow[:, hs]).astype(BF16)
            b_out[h] = dot(sq, grad, TN).astype(BF16)
        for j in range(group):
            spread_head(b_out, b_in, b_s, b_r, far_first(g * group + j))
        return 0

    lax.fori_loop(0, steps, adjoints, 0)
    keep(b_out, b_in)

    def inside_grads(g, _):
        for j in range(group):
            h = g * group + j
            hs = lanes(h)
            grad = ag[:, hs]
            sg = (dot(grad, v_ref[:, hs], NT) * mix[h]).astype(BF16)
            qg = dot(sg, kc[:, hs], NN) + grow[:, hs] * dot(grad, whole(p_in, h), NT)
            acc[:, hs] = qg + dot(wts[h], grad, TN)
            ckg[pl.ds(0, toks), hs] = dot(sg, q_ref[:, hs], TN)
        return 0

    lax.fori_loop(0, steps, inside_grads, 0)
    scan(b_in, b_r, a_out, a_in, a_s, a_r, range(ctx_n - 1, -1, -1))

    def edge(h):
        hs = lanes(h)
        return remote(
            ckg.at[pl.ds(0, HALO), hs], ckg.at[pl.ds(toks, HALO), hs], ch_s.at[h], ch_r.at[h],
            {"ctx": lax.rem(ctx + ctx_n - 1, ctx_n)},
        )

    def outside_grads(g, _):
        for j in range(group):
            collect(a_in, a_r, near_first(g * group + j))
        for j in range(group):
            h = near_first(g * group + j)
            hs = lanes(h)
            wa = after[:, hs]
            state = whole(a_in, h)
            ckg[pl.ds(0, toks), hs] += wa * dot(v_ref[:, hs], state, NT)
            acc[:, hs] += wa * dot(kc[:, hs], state, NN)

        @pl.when(ctx > 0)
        def _():
            for j in range(group):
                edge(near_first(g * group + j)).start()

        return 0

    lax.fori_loop(0, steps, outside_grads, 0)

    def back(h):
        hs = lanes(h)
        return remote(
            gst.at[:, hs], gin_ref.at[:, hs], pp_s.at[h], pp_r.at[h],
            {"pp": lax.rem(pp + pp_n - 1, pp_n)},
        )

    def finish(g, _):
        @pl.when(ctx < ctx_n - 1)
        def _():
            for j in range(group):
                edge(near_first(g * group + j)).wait_recv()

        for j in range(group):
            h = near_first(g * group + j)
            hs = lanes(h)
            total = acc[:, hs]
            for tap in range(taps):
                total = total + w_ref[pl.ds(tap, 1), hs] * ckg[pl.ds(tap, toks), hs]
            gst[:, hs] = total.astype(BF16)

        @pl.when(pp > 0)
        def _():
            for j in range(group):
                back(near_first(g * group + j)).start()

        return 0

    lax.fori_loop(0, steps, finish, 0)

    @pl.when(ctx < ctx_n - 1)
    def _():
        halo.wait_send()

    for step in range(1, tp_n):
        sums(step).wait_send()

    def left(step, _):
        peer = lax.rem(ctx + step, ctx_n)
        total_to(step).wait_send()
        h, part = peer // parts, lax.rem(peer, parts)
        spread(s_out, s_in, s_s, s_r, h, part).wait_send()
        spread(b_out, b_in, b_s, b_r, h, part).wait_send()
        deliver(p_out, p_in, p_s, p_r, peer).wait_send()
        deliver(a_out, a_in, a_s, a_r, peer).wait_send()
        return 0

    lax.fori_loop(1, ctx_n, left, 0)

    @pl.when(ctx > 0)
    def _():
        def leave(h, _):
            edge(h).wait_send()
            return 0

        lax.fori_loop(0, heads, leave, 0)

    @pl.when(pp > 0)
    def _():
        def leave(h, _):
            back(h).wait_send()
            return 0

        lax.fori_loop(0, heads, leave, 0)

    @pl.when(pp < pp_n - 1)
    def _():
        def land(h, _):
            back(h).wait_recv()
            return 0

        lax.fori_loop(0, heads, land, 0)


def solution(mesh):
    ctx_n, tp_n, pp_n = mesh.shape["ctx"], mesh.shape["tp"], mesh.shape["pp"]

    def per_device(queries, key_input, values, log_decay, conv_weight, out_grad):
        toks, feats = queries.shape[1:]
        heads = log_decay.shape[2]
        hd = feats // heads
        parts = ctx_n // heads
        rows = -(-hd // (16 * parts)) * 16
        dma = pltpu.SemaphoreType.DMA
        flat_b = pltpu.VMEM((toks, feats), BF16)
        flat_f = pltpu.VMEM((toks, feats), F32)
        states = pltpu.VMEM((heads, hd, hd), BF16)
        shares = pltpu.VMEM((ctx_n, rows, hd), BF16)
        longer = pltpu.VMEM((toks + HALO, feats), F32)
        square = pltpu.VMEM((toks, hd), F32)
        scratch = [
            flat_b, flat_b, flat_b, flat_b, pltpu.VMEM((16, feats), BF16), longer, flat_b,
            flat_f, flat_f, pltpu.VMEM((heads, toks, toks), F32),
            pltpu.VMEM((heads, toks, toks), BF16), flat_f, flat_b, flat_f, longer, flat_b,
            pltpu.VMEM((heads, 1, hd), F32), pltpu.VMEM((ctx_n, 1, hd), F32), square, square,
            pltpu.VMEM((tp_n, 8, toks), F32),
            states, shares, shares, shares, states, shares, shares, shares,
            dma((4,)), dma, dma, dma((ctx_n - 1,)), dma((ctx_n - 1,)),
            dma((tp_n - 1,)), dma((tp_n - 1,)),
        ]
        scratch += [dma((ctx_n,))] * 8 + [dma((heads,))] * 4
        whole = pl.BlockSpec(memory_space=pltpu.VMEM)
        there = pl.BlockSpec(memory_space=pl.ANY)

        def body(*refs):
            kernel(ctx_n, tp_n, pp_n, *refs)

        shape = jax.ShapeDtypeStruct((toks, feats), BF16)
        out, gin = pl.pallas_call(
            body,
            out_shape=(shape, shape),
            in_specs=[there, there, there, whole, whole, there],
            out_specs=(whole, whole),
            scratch_shapes=scratch,
            compiler_params=pltpu.CompilerParams(
                collective_id=0, has_side_effects=True, vmem_limit_bytes=63 * 1024 * 1024
            ),
        )(
            queries[0], key_input[0], values[0], log_decay[0].T, conv_weight[0], out_grad[0]
        )
        return out[None], gin[None]

    placed = (
        P("pp", "ctx", "tp"),
        P("pp", "ctx", "tp"),
        P("pp", "ctx", "tp"),
        P("pp", "ctx", "tp"),
        P("pp", None, "tp"),
        P("pp", "ctx", "tp"),
    )
    return jax.shard_map(
        per_device,
        mesh=mesh,
        in_specs=placed,
        out_specs=(P("pp", "ctx", "tp"), P("pp", "ctx", "tp")),
        check_vma=False,
    )
```

time: 115 us -> 88.6 us (0.77)
  Pallas kernels: 107 us -> 85.3 us
  local copies, waits for them, and re-layouts: 6.6 us -> 2.42 us
    pallas_call x1, Pallas kernels: 107 us -> 85.3 us  [per_device(): pl.pallas_call(body, out_shape=(shape, shape), in_specs=[there, there, th...]
    unnamed x15 -> x4, local copies, waits for them, and re-layouts: 6.6 us -> 2.42 us
where the time goes in v2:
time: 88.6 us; the launch traced here: 88.4 us
  Pallas kernels  85.3 us (96%)
  local copies, waits for them, and re-layouts  2.42 us (3%)
    pallas_call x1, Pallas kernels, per_device(): pl.pallas_call(body, out_shape=(shape, shape), in_specs=[there, there, th...  85.3 us
    unnamed x4, local copies, waits for them, and re-layouts  2.42 us

profile of v2, /device:TPU:25, one launch (start us, length us, event | category | flops | bytes accessed | tf_op | source)
XLA Modules:
  0.0 88.4 jit_solution(13935862411068478731)
XLA Ops:
  0.6 85.3 %shard_map.77 = (bf16[128,1024]{1,0:T(8,128)(2,1)}, bf16[128,1024]{1,0:T(8,128)(2,1)}) custom-call(bf16[128,1024]{1,0:T(8,128)(2,1)} %bitcast.12, bf16[128,1024]{1,0:T(8,128)(2,1)} %bitcast.13, bf16[128,1024]{1,0:T(8,128)(2,1)} %bitcast.14, f32[8,128]{1,0:T(8,128)} %bitcast.17, f32[4,1024]{1,0:T(4,128)} %bitcast.16, bf16[128,1024]{1,0:T(8,128)(2,1)} %bitcast.15), custom_call_target="tpu_custom_call" | custom-call | tf_op jit(solution)/shard_map/pallas_call | solution.py:464
  86.0 0.0 copy-start
  86.0 1.7 %copy.10 = bf16[1,128,1024]{2,1,0:T(8,128)(2,1)} copy(bf16[1,128,1024]{2,1,0:T(8,128)(2,1)} %bitcast.11) | data formatting | bytes 524288
  87.7 0.0 copy-done
  87.7 0.7 copy.11
Async XLA Ops:
  86.0 1.7 %copy-start = (bf16[128,1024]{1,0:T(8,128)(2,1)S(1)}, bf16[128,1024]{1,0:T(8,128)(2,1)}, u32[]{:S(2)}) copy-start(bf16[128,1024]{1,0:T(8,128)(2,1)} %get-tuple-element.5) | copy-start | bytes 786436

commit v3 on v2

--- a/solution.py
+++ b/solution.py
@@ -37,10 +37,12 @@
     q_hbm, k_hbm, v_hbm, ld_ref, w_ref, og_hbm,
     out_ref, gin_ref,
     q_ref, k_ref, v_ref, og_ref, halo_ref, kext, kc, grow, after, mix, wts, att, ag, acc, ckg, gst,
-    bt, bt_all, acc_sq, acc_dot, tpbuf,
-    s_out, s_in, p_out, p_in, b_out, b_in, a_out, a_in,
-    load_sem, halo_s, halo_r, bt_s, bt_r, tp_s, tp_r,
-    s_s, s_r, p_s, p_r, b_s, b_r, a_s, a_r, ch_s, ch_r, pp_s, pp_r,
+    bt, bt_p, bt_all, acc_sq, acc_dot, tpbuf,
+    s_m, s_t, s_out, s_in, p_out, p_in, p_half, p_stage,
+    b_m, b_t, b_out, b_in, a_out, a_in, a_half, a_stage,
+    load_sem, halo_s, halo_r, bp_s, bp_r, bt_s, bt_r, tp_s, tp_r,
+    s_s, s_r, p_s, p_r, b_s, b_r, a_s, a_r,
+    sx_s, sx_r, px_s, px_r, bx_s, bx_r, ax_s, ax_r, ch_s, ch_r, pp_s, pp_r,
 ):
     toks, feats = q_hbm.shape
     heads = ld_ref.shape[0]
@@ -49,29 +51,41 @@
     width_all = feats * tp_n
     parts = ctx_n // heads
     rows = s_in.shape[1]
-    group = min(GROUP, heads)
+    short = hd - rows * (parts - 1)
+    group = min(GROUP, heads // 2)
     steps = heads // group
+    half = heads // 2
+    half_steps = half // group
+    chips = ctx_n // 2
     ctx = lax.axis_index("ctx")
     tp = lax.axis_index("tp")
     pp = lax.axis_index("pp")
+    core = lax.rem(ctx, 2)
+    chip = ctx // 2
+    partner = ctx + 1 - 2 * core
+    own0 = half * core
+    their0 = half * (1 - core)
     my_head = ctx // parts
     my_part = lax.rem(ctx, parts)
-    far_head = lax.rem(ctx + ctx_n // 2, ctx_n) // parts
+    scan_core = my_head // half
 
     def lanes(h):
         return pl.ds(pl.multiple_of(h * hd, hd), hd)
 
-    def begin(part):
-        return part * rows - (part // (parts - 1)) * (parts * rows - hd)
-
     def fan(idx):
         return ((idx + 1) // 2) * (2 * lax.rem(idx, 2) - 1)
 
-    def far_first(idx):
-        return lax.rem(far_head + fan(idx) + heads, heads)
-
-    def near_first(idx):
-        return lax.rem(my_head + fan(idx) + heads, heads)
+    def carried(side, n):
+        place = lax.rem(2 * chip + side - chips * side + ctx_n, ctx_n)
+        down = 1 - lax.rem(place + ctx_n // 4, ctx_n) // chips
+        return n + down * (half - 1 - 2 * n)
+
+    def own_first(idx):
+        side = core + (idx // half) * (1 - 2 * core)
+        return half * side + carried(side, lax.rem(idx, half))
+
+    def own_last(idx):
+        return own_first(lax.rem(idx + half, heads))
 
     barrier = pltpu.get_barrier_semaphore()
     greet = [{"ctx": lax.rem(ctx + step, ctx_n)} for step in range(1, ctx_n)]
@@ -158,67 +172,143 @@
 
     kext[pl.ds(0, HALO), :] = halo_ref[pl.ds(tail - HALO, HALO), :].astype(F32)
 
-    def spread(src, dst, send_sem, recv_sem, h, part):
-        owner = h * parts + part
-        first = pl.multiple_of(begin(part), 16)
-        return remote(
-            src.at[h, pl.ds(first, rows)], dst.at[ctx], send_sem.at[owner], recv_sem.at[ctx],
-            {"ctx": owner},
-        )
-
-    def spread_head(src, dst, send_sem, recv_sem, h):
-        for part in range(parts):
-            @pl.when(h * parts + part != ctx)
+    swap_bt = remote(bt, bt_p, bp_s, bp_r, {"ctx": partner})
+    swap_bt.start()
+
+    def sized(call):
+        @pl.when(my_part < parts - 1)
+        def _():
+            call(rows)
+
+        @pl.when(my_part == parts - 1)
+        def _():
+            call(short)
+
+    if short < rows:
+        @pl.when(my_part == parts - 1)
+        def _():
+            s_in[:, pl.ds(short, rows - short), :] = jnp.zeros((chips, rows - short, hd), BF16)
+            b_in[:, pl.ds(short, rows - short), :] = jnp.zeros((chips, rows - short, hd), BF16)
+
+    def swap(mine, theirs, send_sem, recv_sem, i):
+        return remote(
+            mine.at[their0 + i], theirs.at[i], send_sem.at[i], recv_sem.at[i], {"ctx": partner}
+        )
+
+    def spread(src, dst, send_sem, recv_sem, i, part):
+        size = rows if part < parts - 1 else short
+        return remote(
+            src.at[i, pl.ds(part * rows, size)], dst.at[chip, pl.ds(0, size)],
+            send_sem.at[i * parts + part], recv_sem.at[chip],
+            {"ctx": (own0 + i) * parts + part},
+        )
+
+    def deliver(src, dst, send_sem, recv_sem, z, size):
+        slot = ctx - scan_core * chips
+        return remote(
+            src.at[z, pl.ds(0, size)], dst.at[slot, pl.ds(0, size)], send_sem.at[z],
+            recv_sem.at[slot], {"ctx": 2 * z + scan_core},
+        )
+
+    def arrive(dst, recv_sem, n, size):
+        piece = dst.at[n, pl.ds(0, size)]
+        return remote(piece, piece, recv_sem.at[n], recv_sem.at[n], {"ctx": partner})
+
+    def factors(h, lead):
+        e_m = jnp.exp(bt[h])
+        e_t = jnp.exp(bt_p[h])
+        return e_m, e_t, lead.astype(F32)
+
+    def join(mine, theirs, xs, xr, out, into, send_sem, recv_sem, lead):
+        def one(n, _):
+            i = carried(core, n)
+            h = own0 + i
+            e_m, e_t, lf = factors(h, lead)
+            swap(mine, theirs, xs, xr, i).wait_recv()
+            ca = lf * e_t + (1.0 - lf)
+            cb = lf + (1.0 - lf) * e_m
+            out[i] = (ca * mine[h] + cb * theirs[i]).astype(BF16)
+            for part in range(parts):
+                @pl.when(h * parts + part != ctx)
+                def _():
+                    spread(out, into, send_sem, recv_sem, i, part).start()
+
+                @pl.when(h * parts + part == ctx)
+                def _():
+                    size = rows if part < parts - 1 else short
+                    into[chip, pl.ds(0, size), :] = out[i, pl.ds(part * rows, size), :]
+            return 0
+
+        lax.fori_loop(0, half, one, 0)
+
+    def scan(into, recv_sem, out, home, send_sem, home_sem, order):
+        def ready(z, _):
+            @pl.when(2 * z + scan_core != ctx)
             def _():
-                spread(src, dst, send_sem, recv_sem, h, part).start()
-
-    def keep(src, dst):
-        dst[ctx] = src[my_head, pl.ds(pl.multiple_of(begin(my_part), 16), rows), :]
-
-    def deliver(src, dst, send_sem, recv_sem, c):
-        return remote(
-            src.at[c], dst.at[ctx], send_sem.at[c], recv_sem.at[ctx], {"ctx": c}
-        )
-
-    def arrive(src, recv_sem, n):
-        return remote(src.at[n], src.at[n], recv_sem.at[n], recv_sem.at[n], {"ctx": ctx})
-
-    def scan(into, recv_sem, out, home, send_sem, home_sem, order):
-        def ready(step, _):
-            n = lax.rem(ctx + step, ctx_n)
-            arrive(into, recv_sem, n).wait_recv()
+                sized(lambda size: arrive(into, recv_sem, z, size).wait_recv())
+
             return 0
 
-        lax.fori_loop(1, ctx_n, ready, 0)
+        lax.fori_loop(0, chips, ready, 0)
         carry = jnp.zeros((rows, hd), F32)
-        for c in order:
-            out[c] = carry.astype(BF16)
-            carry = jnp.exp(bt_all[c]) * carry + into[c].astype(F32)
+        for z in order:
+            out[z] = carry.astype(BF16)
+            carry = jnp.exp(bt_all[2 * z] + bt_all[2 * z + 1]) * carry + into[z].astype(F32)
 
         def give(idx, _):
-            c = lax.rem(ctx + ctx_n // 2 + fan(idx) + ctx_n, ctx_n)
-            deliver(out, home, send_sem, home_sem, c).start()
+            z = lax.rem(chip + chips // 2 + fan(idx) + chips, chips)
+
+            @pl.when(2 * z + scan_core != ctx)
+            def _():
+                sized(lambda size: deliver(out, home, send_sem, home_sem, z, size).start())
+
             return 0
 
-        lax.fori_loop(0, ctx_n - 1, give, 0)
-        home[ctx] = out[ctx]
-
-    def collect(home, home_sem, h):
-        for part in range(parts):
-            @pl.when(h * parts + part != ctx)
-            def _():
-                arrive(home, home_sem, h * parts + part).wait_recv()
-
-    def whole(home, h):
-        pieces = []
-        for part in range(parts):
-            piece = home[h * parts + part]
-            pieces.append(piece[part * rows - begin(part) :, :])
-        return jnp.concatenate(pieces, axis=0)
+        lax.fori_loop(0, chips, give, 0)
+
+        @pl.when(scan_core == core)
+        def _():
+            home[ctx - scan_core * chips] = out[chip]
+
+    def hand(stage, dest, send_sem, recv_sem, i, h):
+        return remote(
+            stage.at[i], dest.at[h], send_sem.at[i], recv_sem.at[i], {"ctx": partner}
+        )
+
+    def split(home, home_sem, mine, theirs, dest, stage, hs_, hr_, lead):
+        def one(n, _):
+            i = carried(core, n)
+            h = own0 + i
+            e_m, e_t, lf = factors(h, lead)
+            pieces = []
+            for part in range(parts):
+                size = rows if part < parts - 1 else short
+
+                @pl.when(h * parts + part != ctx)
+                def _():
+                    arrive(home, home_sem, i * parts + part, size).wait_recv()
+
+                pieces.append(home[i * parts + part, pl.ds(0, size), :].astype(F32))
+            carry = jnp.concatenate(pieces, axis=0)
+            c1 = lf + (1.0 - lf) * e_t
+            c2 = lf * e_m + (1.0 - lf)
+            stage[i] = (c2 * carry + lf * mine[h]).astype(BF16)
+            hand(stage, dest, hs_, hr_, i, h).start()
+            dest[h] = (c1 * carry + (1.0 - lf) * theirs[i]).astype(BF16)
+            return 0
+
+        lax.fori_loop(0, half, one, 0)
+
+    def handed(stage, dest, hs_, hr_, g):
+        @pl.when(g >= half_steps)
+        def _():
+            for j in range(group):
+                h = own_first(g * group + j)
+                hand(stage, dest, hs_, hr_, h - their0, h).wait_recv()
 
     def states(g, _):
         for j in range(group):
-            h = far_first(g * group + j)
+            h = own_last(g * group + j)
             hs = lanes(h)
             conv = w_ref[pl.ds(0, 1), hs] * kext[pl.ds(HALO, toks), hs]
             for tap in range(1, taps):
@@ -226,13 +316,18 @@
             keys = conv.astype(BF16)
             kc[:, hs] = keys
             scaled = (keys.astype(F32) * after[:, hs]).astype(BF16)
-            s_out[h] = dot(scaled, v_ref[:, hs], TN).astype(BF16)
-        for j in range(group):
-            spread_head(s_out, s_in, s_s, s_r, far_first(g * group + j))
+            s_m[h] = dot(scaled, v_ref[:, hs], TN)
+
+        @pl.when(g < half_steps)
+        def _():
+            for j in range(group):
+                swap(s_m, s_t, sx_s, sx_r, own_last(g * group + j) - their0).start()
+
         return 0
 
     lax.fori_loop(0, steps, states, 0)
-    keep(s_out, s_in)
+    swap_bt.wait_recv()
+    join(s_m, s_t, sx_s, sx_r, s_out, s_in, s_s, s_r, core == 0)
     loads[2].wait()
 
     def inside(g, _):
@@ -252,19 +347,19 @@
         return 0
 
     lax.fori_loop(1, ctx_n, total_in, 0)
-    scan(s_in, s_r, p_out, p_in, p_s, p_r, range(ctx_n))
+    scan(s_in, s_r, p_out, p_in, p_s, p_r, range(chips))
+    split(p_in, p_r, s_m, s_t, p_half, p_stage, px_s, px_r, core == 0)
 
     loads[3].wait()
     acc_sq[...] = jnp.zeros_like(acc_sq)
     acc_dot[...] = jnp.zeros_like(acc_dot)
 
     def attend(g, _):
+        handed(p_stage, p_half, px_s, px_r, g)
         for j in range(group):
-            collect(p_in, p_r, near_first(g * group + j))
-        for j in range(group):
-            h = near_first(g * group + j)
+            h = own_first(g * group + j)
             hs = lanes(h)
-            a = att[:, hs] + grow[:, hs] * dot(q_ref[:, hs], whole(p_in, h), NN)
+            a = att[:, hs] + grow[:, hs] * dot(q_ref[:, hs], p_half[h], NN)
             att[:, hs] = a
             acc_sq[...] += a * a
             acc_dot[...] += a * og_ref[:, hs].astype(F32)
@@ -297,20 +392,24 @@
 
     def adjoints(g, _):
         for j in range(group):
-            h = far_first(g * group + j)
+            h = own_last(g * group + j)
             hs = lanes(h)
             normed = att[:, hs] * inv
             out_ref[:, hs] = normed.astype(BF16)
             grad = ((og_ref[:, hs].astype(F32) - normed * shift) * inv).astype(BF16)
             ag[:, hs] = grad
             sq = (q_ref[:, hs].astype(F32) * grow[:, hs]).astype(BF16)
-            b_out[h] = dot(sq, grad, TN).astype(BF16)
-        for j in range(group):
-            spread_head(b_out, b_in, b_s, b_r, far_first(g * group + j))
+            b_m[h] = dot(sq, grad, TN)
+
+        @pl.when(g < half_steps)
+        def _():
+            for j in range(group):
+                swap(b_m, b_t, bx_s, bx_r, own_last(g * group + j) - their0).start()
+
         return 0
 
     lax.fori_loop(0, steps, adjoints, 0)
-    keep(b_out, b_in)
+    join(b_m, b_t, bx_s, bx_r, b_out, b_in, b_s, b_r, core == 1)
 
     def inside_grads(g, _):
         for j in range(group):
@@ -318,13 +417,14 @@
             hs = lanes(h)
             grad = ag[:, hs]
             sg = (dot(grad, v_ref[:, hs], NT) * mix[h]).astype(BF16)
-            qg = dot(sg, kc[:, hs], NN) + grow[:, hs] * dot(grad, whole(p_in, h), NT)
+            qg = dot(sg, kc[:, hs], NN) + grow[:, hs] * dot(grad, p_half[h], NT)
             acc[:, hs] = qg + dot(wts[h], grad, TN)
             ckg[pl.ds(0, toks), hs] = dot(sg, q_ref[:, hs], TN)
         return 0
 
     lax.fori_loop(0, steps, inside_grads, 0)
-    scan(b_in, b_r, a_out, a_in, a_s, a_r, range(ctx_n - 1, -1, -1))
+    scan(b_in, b_r, a_out, a_in, a_s, a_r, range(chips - 1, -1, -1))
+    split(a_in, a_r, b_m, b_t, a_half, a_stage, ax_s, ax_r, core == 1)
 
     def edge(h):
         hs = lanes(h)
@@ -334,20 +434,19 @@
         )
 
     def outside_grads(g, _):
+        handed(a_stage, a_half, ax_s, ax_r, g)
         for j in range(group):
-            collect(a_in, a_r, near_first(g * group + j))
-        for j in range(group):
-            h = near_first(g * group + j)
+            h = own_first(g * group + j)
             hs = lanes(h)
             wa = after[:, hs]
-            state = whole(a_in, h)
+            state = a_half[h]
             ckg[pl.ds(0, toks), hs] += wa * dot(v_ref[:, hs], state, NT)
             acc[:, hs] += wa * dot(kc[:, hs], state, NN)
 
         @pl.when(ctx > 0)
         def _():
             for j in range(group):
-                edge(near_first(g * group + j)).start()
+                edge(own_first(g * group + j)).start()
 
         return 0
 
@@ -364,10 +463,10 @@
         @pl.when(ctx < ctx_n - 1)
         def _():
             for j in range(group):
-                edge(near_first(g * group + j)).wait_recv()
+                edge(own_first(g * group + j)).wait_recv()
 
         for j in range(group):
-            h = near_first(g * group + j)
+            h = own_first(g * group + j)
             hs = lanes(h)
             total = acc[:, hs]
             for tap in range(taps):
@@ -377,7 +476,7 @@
         @pl.when(pp > 0)
         def _():
             for j in range(group):
-                back(near_first(g * group + j)).start()
+                back(own_first(g * group + j)).start()
 
         return 0
 
@@ -390,17 +489,38 @@
     for step in range(1, tp_n):
         sums(step).wait_send()
 
-    def left(step, _):
-        peer = lax.rem(ctx + step, ctx_n)
+    swap_bt.wait_send()
+
+    def told(step, _):
         total_to(step).wait_send()
-        h, part = peer // parts, lax.rem(peer, parts)
-        spread(s_out, s_in, s_s, s_r, h, part).wait_send()
-        spread(b_out, b_in, b_s, b_r, h, part).wait_send()
-        deliver(p_out, p_in, p_s, p_r, peer).wait_send()
-        deliver(a_out, a_in, a_s, a_r, peer).wait_send()
-        return 0
-
-    lax.fori_loop(1, ctx_n, left, 0)
+        return 0
+
+    lax.fori_loop(1, ctx_n, told, 0)
+
+    def left(i, _):
+        h = own0 + i
+        swap(s_m, s_t, sx_s, sx_r, i).wait_send()
+        swap(b_m, b_t, bx_s, bx_r, i).wait_send()
+        hand(p_stage, p_half, px_s, px_r, i, h).wait_send()
+        hand(a_stage, a_half, ax_s, ax_r, i, h).wait_send()
+        for part in range(parts):
+            @pl.when(h * parts + part != ctx)
+            def _():
+                spread(s_out, s_in, s_s, s_r, i, part).wait_send()
+                spread(b_out, b_in, b_s, b_r, i, part).wait_send()
+        return 0
+
+    lax.fori_loop(0, half, left, 0)
+
+    def given(z, _):
+        @pl.when(2 * z + scan_core != ctx)
+        def _():
+            sized(lambda size: deliver(p_out, p_in, p_s, p_r, z, size).wait_send())
+            sized(lambda size: deliver(a_out, a_in, a_s, a_r, z, size).wait_send())
+
+        return 0
+
+    lax.fori_loop(0, chips, given, 0)
 
     @pl.when(ctx > 0)
     def _():
@@ -439,21 +559,28 @@
         dma = pltpu.SemaphoreType.DMA
         flat_b = pltpu.VMEM((toks, feats), BF16)
         flat_f = pltpu.VMEM((toks, feats), F32)
-        states = pltpu.VMEM((heads, hd, hd), BF16)
-        shares = pltpu.VMEM((ctx_n, rows, hd), BF16)
+        half = heads // 2
+        chips = ctx_n // 2
+        full_f = pltpu.VMEM((heads, hd, hd), F32)
+        full_b = pltpu.VMEM((heads, hd, hd), BF16)
+        half_f = pltpu.VMEM((half, hd, hd), F32)
+        half_b = pltpu.VMEM((half, hd, hd), BF16)
+        shares = pltpu.VMEM((chips, rows, hd), BF16)
+        totals = pltpu.VMEM((heads, 1, hd), F32)
+        scanned = [full_f, half_f, half_b, shares, shares, shares, full_b, half_b]
         longer = pltpu.VMEM((toks + HALO, feats), F32)
         square = pltpu.VMEM((toks, hd), F32)
         scratch = [
             flat_b, flat_b, flat_b, flat_b, pltpu.VMEM((16, feats), BF16), longer, flat_b,
             flat_f, flat_f, pltpu.VMEM((heads, toks, toks), F32),
             pltpu.VMEM((heads, toks, toks), BF16), flat_f, flat_b, flat_f, longer, flat_b,
-            pltpu.VMEM((heads, 1, hd), F32), pltpu.VMEM((ctx_n, 1, hd), F32), square, square,
+            totals, totals, pltpu.VMEM((ctx_n, 1, hd), F32), square, square,
             pltpu.VMEM((tp_n, 8, toks), F32),
-            states, shares, shares, shares, states, shares, shares, shares,
-            dma((4,)), dma, dma, dma((ctx_n - 1,)), dma((ctx_n - 1,)),
-            dma((tp_n - 1,)), dma((tp_n - 1,)),
         ]
-        scratch += [dma((ctx_n,))] * 8 + [dma((heads,))] * 4
+        scratch += scanned + scanned
+        scratch += [dma((4,)), dma, dma, dma, dma, dma((ctx_n - 1,)), dma((ctx_n - 1,))]
+        scratch += [dma((max(tp_n - 1, 1),))] * 2 + [dma((chips,))] * 8 + [dma((half,))] * 8
+        scratch += [dma((heads,))] * 4
         whole = pl.BlockSpec(memory_space=pltpu.VMEM)
         there = pl.BlockSpec(memory_space=pl.ANY)
 

time: 88.6 us -> 76.2 us (0.86)
  Pallas kernels: 85.3 us -> 72.9 us
    pallas_call x1, Pallas kernels: 85.3 us -> 72.9 us  [per_device(): pl.pallas_call(body, out_shape=(shape, shape), in_specs=[there, there, th...]
where the time goes in v3:
time: 76.2 us; the launch traced here: 76 us
  Pallas kernels  72.9 us (96%)
  local copies, waits for them, and re-layouts  2.42 us (3%)
    pallas_call x1, Pallas kernels, per_device(): pl.pallas_call(body, out_shape=(shape, shape), in_specs=[there, there, th...  72.9 us
    unnamed x4, local copies, waits for them, and re-layouts  2.42 us

profile of v3, /device:TPU:25, one launch (start us, length us, event | category | flops | bytes accessed | tf_op | source)
XLA Modules:
  0.0 76.0 jit_solution(4062698641626438247)
XLA Ops:
  0.6 72.9 %shard_map.77 = (bf16[128,1024]{1,0:T(8,128)(2,1)}, bf16[128,1024]{1,0:T(8,128)(2,1)}) custom-call(bf16[128,1024]{1,0:T(8,128)(2,1)} %bitcast.12, bf16[128,1024]{1,0:T(8,128)(2,1)} %bitcast.13, bf16[128,1024]{1,0:T(8,128)(2,1)} %bitcast.14, f32[8,128]{1,0:T(8,128)} %bitcast.17, f32[4,1024]{1,0:T(4,128)} %bitcast.16, bf16[128,1024]{1,0:T(8,128)(2,1)} %bitcast.15), custom_call_target="tpu_custom_call" | custom-call | tf_op jit(solution)/shard_map/pallas_call | solution.py:591
  73.5 0.0 copy-start
  73.5 1.7 %copy.10 = bf16[1,128,1024]{2,1,0:T(8,128)(2,1)} copy(bf16[1,128,1024]{2,1,0:T(8,128)(2,1)} %bitcast.11) | data formatting | bytes 524288
  75.2 0.0 copy-done
  75.2 0.7 copy.11
Async XLA Ops:
  73.5 1.7 %copy-start = (bf16[128,1024]{1,0:T(8,128)(2,1)S(1)}, bf16[128,1024]{1,0:T(8,128)(2,1)}, u32[]{:S(2)}) copy-start(bf16[128,1024]{1,0:T(8,128)(2,1)} %get-tuple-element.5) | copy-start | bytes 786436

commit v4 on v3

--- a/solution.py
+++ b/solution.py
@@ -37,10 +37,10 @@
     q_hbm, k_hbm, v_hbm, ld_ref, w_ref, og_hbm,
     out_ref, gin_ref,
     q_ref, k_ref, v_ref, og_ref, halo_ref, kext, kc, grow, after, mix, wts, att, ag, acc, ckg, gst,
-    bt, bt_p, bt_all, acc_sq, acc_dot, tpbuf,
+    bt, bt_p, tot, bt_all, acc_sq, acc_dot, tpbuf,
     s_m, s_t, s_out, s_in, p_out, p_in, p_half, p_stage,
     b_m, b_t, b_out, b_in, a_out, a_in, a_half, a_stage,
-    load_sem, halo_s, halo_r, bp_s, bp_r, bt_s, bt_r, tp_s, tp_r,
+    here, load_sem, halo_s, halo_r, bp_s, bp_r, bt_s, bt_r, tp_s, tp_r,
     s_s, s_r, p_s, p_r, b_s, b_r, a_s, a_r,
     sx_s, sx_r, px_s, px_r, bx_s, bx_r, ax_s, ax_r, ch_s, ch_r, pp_s, pp_r,
 ):
@@ -72,28 +72,34 @@
     def lanes(h):
         return pl.ds(pl.multiple_of(h * hd, hd), hd)
 
-    def fan(idx):
-        return ((idx + 1) // 2) * (2 * lax.rem(idx, 2) - 1)
-
-    def carried(side, n):
-        place = lax.rem(2 * chip + side - chips * side + ctx_n, ctx_n)
-        down = 1 - lax.rem(place + ctx_n // 4, ctx_n) // chips
-        return n + down * (half - 1 - 2 * n)
-
     def own_first(idx):
-        side = core + (idx // half) * (1 - 2 * core)
-        return half * side + carried(side, lax.rem(idx, half))
+        return lax.rem(own0 + idx, heads)
 
     def own_last(idx):
-        return own_first(lax.rem(idx + half, heads))
+        return lax.rem(their0 + idx, heads)
 
     barrier = pltpu.get_barrier_semaphore()
-    greet = [{"ctx": lax.rem(ctx + step, ctx_n)} for step in range(1, ctx_n)]
+    greet = [{"ctx": partner}]
     greet += [{"tp": lax.rem(tp + step, tp_n)} for step in range(1, tp_n)]
-    if pp_n > 1:
-        greet += [{"pp": lax.rem(pp + step, pp_n)} for step in (1, pp_n - 1)]
     for where in greet:
         pl.semaphore_signal(barrier, inc=1, device_id=where, device_id_type=MESH)
+
+    @pl.when(pp < pp_n - 1)
+    def _():
+        pl.semaphore_signal(
+            barrier, inc=1, device_id={"pp": lax.rem(pp + 1, pp_n)}, device_id_type=MESH
+        )
+
+    def enter(peer, _):
+        pl.semaphore_signal(barrier, inc=1, device_id={"ctx": peer}, device_id_type=MESH)
+        return 0
+
+    lax.fori_loop(2 * chip + 2, ctx_n, enter, 0)
+
+    def meet(z):
+        @pl.when(jnp.logical_and(z > chip, z != chip + core))
+        def _():
+            pl.semaphore_wait(here.at[z], 2)
 
     loads = [
         pltpu.make_async_copy(src, dst, load_sem.at[n])
@@ -103,6 +109,14 @@
     ]
     for load in loads:
         load.start()
+
+    pl.semaphore_wait(barrier, len(greet) + 2 * chip + (pp + pp_n - 1) // pp_n)
+
+    def answer(peer, _):
+        pl.semaphore_signal(here.at[chip], inc=1, device_id={"ctx": peer}, device_id_type=MESH)
+        return 0
+
+    lax.fori_loop(0, 2 * chip, answer, 0)
 
     rows_i = lax.broadcasted_iota(jnp.int32, (toks, toks), 0)
     cols_i = lax.broadcasted_iota(jnp.int32, (toks, toks), 1)
@@ -121,10 +135,6 @@
         bt[h] = total
         grow[:, h * hd : (h + 1) * hd] = jnp.exp(wide)
         after[:, h * hd : (h + 1) * hd] = jnp.exp(total - wide)
-        differ = wide - cdt[h : h + 1, :]
-        mix[h] = jnp.where(causal, jnp.exp(jnp.where(causal, differ, 0.0)), 0.0)
-
-    pl.semaphore_wait(barrier, len(greet))
 
     tail = halo_ref.shape[0]
     halo = remote(
@@ -132,23 +142,20 @@
         {"ctx": lax.rem(ctx + 1, ctx_n)},
     )
 
+    @pl.when(jnp.logical_and(core == 1, chip < chips - 1))
+    def _():
+        pl.semaphore_wait(here.at[chip + 1], 2)
+
     @pl.when(ctx < ctx_n - 1)
     def _():
         halo.start()
 
-    def total_to(step):
-        peer = lax.rem(ctx + step, ctx_n)
-        return remote(
-            bt.at[peer // parts], bt_all.at[ctx], bt_s.at[step - 1], bt_r.at[step - 1],
-            {"ctx": peer},
-        )
-
-    def send_total(step, _):
-        total_to(step).start()
-        return 0
-
-    lax.fori_loop(1, ctx_n, send_total, 0)
-    bt_all[ctx] = bt[my_head]
+    swap_bt = remote(bt, bt_p, bp_s, bp_r, {"ctx": partner})
+    swap_bt.start()
+    for h in range(heads):
+        wide = jnp.broadcast_to(cd[:, h : h + 1], (toks, hd))
+        differ = wide - cdt[h : h + 1, :]
+        mix[h] = jnp.where(causal, jnp.exp(jnp.where(causal, differ, 0.0)), 0.0)
 
     @pl.when(ctx == 0)
     def _():
@@ -171,9 +178,6 @@
         halo.wait_recv()
 
     kext[pl.ds(0, HALO), :] = halo_ref[pl.ds(tail - HALO, HALO), :].astype(F32)
-
-    swap_bt = remote(bt, bt_p, bp_s, bp_r, {"ctx": partner})
-    swap_bt.start()
 
     def sized(call):
         @pl.when(my_part < parts - 1)
@@ -219,56 +223,93 @@
         e_t = jnp.exp(bt_p[h])
         return e_m, e_t, lead.astype(F32)
 
-    def join(mine, theirs, xs, xr, out, into, send_sem, recv_sem, lead):
+    def total_to(i, part):
+        return remote(
+            tot.at[i], bt_all.at[chip], bt_s.at[i * parts + part], bt_r.at[chip],
+            {"ctx": (own0 + i) * parts + part},
+        )
+
+    def join(mine, theirs, xs, xr, out, into, send_sem, recv_sem, lead, needed, opening):
         def one(n, _):
-            i = carried(core, n)
+            i = n
             h = own0 + i
             e_m, e_t, lf = factors(h, lead)
             swap(mine, theirs, xs, xr, i).wait_recv()
             ca = lf * e_t + (1.0 - lf)
             cb = lf + (1.0 - lf) * e_m
             out[i] = (ca * mine[h] + cb * theirs[i]).astype(BF16)
+            if opening:
+                tot[i] = bt[h] + bt_p[h]
+                low = (h * parts + 1) // 2
+                high = (h * parts + parts - 1) // 2
+                meet(low)
+
+                @pl.when(high > low)
+                def _():
+                    meet(high)
+
             for part in range(parts):
                 @pl.when(h * parts + part != ctx)
                 def _():
-                    spread(out, into, send_sem, recv_sem, i, part).start()
+                    @pl.when(needed)
+                    def _():
+                        spread(out, into, send_sem, recv_sem, i, part).start()
+
+                    if opening:
+                        total_to(i, part).start()
 
                 @pl.when(h * parts + part == ctx)
                 def _():
                     size = rows if part < parts - 1 else short
                     into[chip, pl.ds(0, size), :] = out[i, pl.ds(part * rows, size), :]
+                    if opening:
+                        bt_all[chip] = tot[i]
             return 0
 
         lax.fori_loop(0, half, one, 0)
 
-    def scan(into, recv_sem, out, home, send_sem, home_sem, order):
-        def ready(z, _):
+    def scan(into, recv_sem, out, home, send_sem, home_sem, opening):
+        def give(z, carry):
+            out[z] = carry.astype(BF16)
+            if opening:
+                late = jnp.where(z >= chips // 2, 1, 0)
+
+                @pl.when(late != core)
+                def _():
+                    meet(z)
+
+            @pl.when(2 * z + scan_core != ctx)
+            def _():
+                sized(lambda size: deliver(out, home, send_sem, home_sem, z, size).start())
+
+            @pl.when(2 * z + scan_core == ctx)
+            def _():
+                home[ctx - scan_core * chips] = out[z]
+
+        def total_in(z):
+            @pl.when(2 * z + scan_core != ctx)
+            def _():
+                remote(
+                    bt_all.at[z], bt_all.at[z], bt_r.at[z], bt_r.at[z], {"ctx": partner}
+                ).wait_recv()
+
+        if not opening:
+            total_in(chips - 1)
+
+        def one(n, carry):
+            z = n if opening else chips - 1 - n
+            give(z, carry)
+            if opening:
+                total_in(z)
+
             @pl.when(2 * z + scan_core != ctx)
             def _():
                 sized(lambda size: arrive(into, recv_sem, z, size).wait_recv())
 
-            return 0
-
-        lax.fori_loop(0, chips, ready, 0)
-        carry = jnp.zeros((rows, hd), F32)
-        for z in order:
-            out[z] = carry.astype(BF16)
-            carry = jnp.exp(bt_all[2 * z] + bt_all[2 * z + 1]) * carry + into[z].astype(F32)
-
-        def give(idx, _):
-            z = lax.rem(chip + chips // 2 + fan(idx) + chips, chips)
-
-            @pl.when(2 * z + scan_core != ctx)
-            def _():
-                sized(lambda size: deliver(out, home, send_sem, home_sem, z, size).start())
-
-            return 0
-
-        lax.fori_loop(0, chips, give, 0)
-
-        @pl.when(scan_core == core)
-        def _():
-            home[ctx - scan_core * chips] = out[chip]
+            return jnp.exp(bt_all[z]) * carry + into[z].astype(F32)
+
+        carry = lax.fori_loop(0, chips - 1, one, jnp.zeros((rows, hd), F32))
+        give(chips - 1 if opening else 0, carry)
 
     def hand(stage, dest, send_sem, recv_sem, i, h):
         return remote(
@@ -277,7 +318,7 @@
 
     def split(home, home_sem, mine, theirs, dest, stage, hs_, hr_, lead):
         def one(n, _):
-            i = carried(core, n)
+            i = n
             h = own0 + i
             e_m, e_t, lf = factors(h, lead)
             pieces = []
@@ -327,7 +368,7 @@
 
     lax.fori_loop(0, steps, states, 0)
     swap_bt.wait_recv()
-    join(s_m, s_t, sx_s, sx_r, s_out, s_in, s_s, s_r, core == 0)
+    join(s_m, s_t, sx_s, sx_r, s_out, s_in, s_s, s_r, core == 0, chip < chips - 1, True)
     loads[2].wait()
 
     def inside(g, _):
@@ -342,12 +383,7 @@
 
     lax.fori_loop(0, steps, inside, 0)
 
-    def total_in(step, _):
-        total_to(step).wait_recv()
-        return 0
-
-    lax.fori_loop(1, ctx_n, total_in, 0)
-    scan(s_in, s_r, p_out, p_in, p_s, p_r, range(chips))
+    scan(s_in, s_r, p_out, p_in, p_s, p_r, True)
     split(p_in, p_r, s_m, s_t, p_half, p_stage, px_s, px_r, core == 0)
 
     loads[3].wait()
@@ -409,7 +445,7 @@
         return 0
 
     lax.fori_loop(0, steps, adjoints, 0)
-    join(b_m, b_t, bx_s, bx_r, b_out, b_in, b_s, b_r, core == 1)
+    join(b_m, b_t, bx_s, bx_r, b_out, b_in, b_s, b_r, core == 1, chip > 0, False)
 
     def inside_grads(g, _):
         for j in range(group):
@@ -423,7 +459,7 @@
         return 0
 
     lax.fori_loop(0, steps, inside_grads, 0)
-    scan(b_in, b_r, a_out, a_in, a_s, a_r, range(chips - 1, -1, -1))
+    scan(b_in, b_r, a_out, a_in, a_s, a_r, False)
     split(a_in, a_r, b_m, b_t, a_half, a_stage, ax_s, ax_r, core == 1)
 
     def edge(h):
@@ -491,12 +527,6 @@
 
     swap_bt.wait_send()
 
-    def told(step, _):
-        total_to(step).wait_send()
-        return 0
-
-    lax.fori_loop(1, ctx_n, told, 0)
-
     def left(i, _):
         h = own0 + i
         swap(s_m, s_t, sx_s, sx_r, i).wait_send()
@@ -506,8 +536,16 @@
         for part in range(parts):
             @pl.when(h * parts + part != ctx)
             def _():
-                spread(s_out, s_in, s_s, s_r, i, part).wait_send()
-                spread(b_out, b_in, b_s, b_r, i, part).wait_send()
+                total_to(i, part).wait_send()
+
+                @pl.when(chip < chips - 1)
+                def _():
+                    spread(s_out, s_in, s_s, s_r, i, part).wait_send()
+
+                @pl.when(chip > 0)
+                def _():
+                    spread(b_out, b_in, b_s, b_r, i, part).wait_send()
+
         return 0
 
     lax.fori_loop(0, half, left, 0)
@@ -574,11 +612,13 @@
             flat_b, flat_b, flat_b, flat_b, pltpu.VMEM((16, feats), BF16), longer, flat_b,
             flat_f, flat_f, pltpu.VMEM((heads, toks, toks), F32),
             pltpu.VMEM((heads, toks, toks), BF16), flat_f, flat_b, flat_f, longer, flat_b,
-            totals, totals, pltpu.VMEM((ctx_n, 1, hd), F32), square, square,
+            totals, totals, pltpu.VMEM((half, 1, hd), F32), pltpu.VMEM((chips, 1, hd), F32),
+            square, square,
             pltpu.VMEM((tp_n, 8, toks), F32),
         ]
         scratch += scanned + scanned
-        scratch += [dma((4,)), dma, dma, dma, dma, dma((ctx_n - 1,)), dma((ctx_n - 1,))]
+        scratch += [pltpu.SemaphoreType.REGULAR((chips,))]
+        scratch += [dma((4,)), dma, dma, dma, dma, dma((chips,)), dma((chips,))]
         scratch += [dma((max(tp_n - 1, 1),))] * 2 + [dma((chips,))] * 8 + [dma((half,))] * 8
         scratch += [dma((heads,))] * 4
         whole = pl.BlockSpec(memory_space=pltpu.VMEM)

time: 76.2 us -> 74.8 us (0.982)
  Pallas kernels: 72.9 us -> 71.5 us
    pallas_call x1, Pallas kernels: 72.9 us -> 71.5 us  [per_device(): pl.pallas_call(body, out_shape=(shape, shape), in_specs=[there, there, th...]
where the time goes in v4:
time: 74.8 us; the launch traced here: 74.6 us
  Pallas kernels  71.5 us (96%)
  local copies, waits for them, and re-layouts  2.42 us (3%)
    pallas_call x1, Pallas kernels, per_device(): pl.pallas_call(body, out_shape=(shape, shape), in_specs=[there, there, th...  71.5 us
    unnamed x4, local copies, waits for them, and re-layouts  2.42 us

profile of v4, /device:TPU:25, one launch (start us, length us, event | category | flops | bytes accessed | tf_op | source)
XLA Modules:
  0.0 74.6 jit_solution(10214703484724145071)
XLA Ops:
  0.6 71.5 %shard_map.77 = (bf16[128,1024]{1,0:T(8,128)(2,1)}, bf16[128,1024]{1,0:T(8,128)(2,1)}) custom-call(bf16[128,1024]{1,0:T(8,128)(2,1)} %bitcast.12, bf16[128,1024]{1,0:T(8,128)(2,1)} %bitcast.13, bf16[128,1024]{1,0:T(8,128)(2,1)} %bitcast.14, f32[8,128]{1,0:T(8,128)} %bitcast.17, f32[4,1024]{1,0:T(4,128)} %bitcast.16, bf16[128,1024]{1,0:T(8,128)(2,1)} %bitcast.15), custom_call_target="tpu_custom_call" | custom-call | tf_op jit(solution)/shard_map/pallas_call | solution.py:631
  72.1 0.0 copy-start
  72.1 1.7 %copy.10 = bf16[1,128,1024]{2,1,0:T(8,128)(2,1)} copy(bf16[1,128,1024]{2,1,0:T(8,128)(2,1)} %bitcast.11) | data formatting | bytes 524288
  73.9 0.0 copy-done
  73.9 0.7 copy.11
Async XLA Ops:
  72.1 1.7 %copy-start = (bf16[128,1024]{1,0:T(8,128)(2,1)S(1)}, bf16[128,1024]{1,0:T(8,128)(2,1)}, u32[]{:S(2)}) copy-start(bf16[128,1024]{1,0:T(8,128)(2,1)} %get-tuple-element.5) | copy-start | bytes 786436

commit v5 on v4

--- a/solution.py
+++ b/solution.py
@@ -9,6 +9,7 @@
 F32 = jnp.float32
 BF16 = jnp.bfloat16
 HALO = 8
+LAST = 16
 GROUP = 2
 
 
@@ -36,13 +37,13 @@
     ctx_n, tp_n, pp_n,
     q_hbm, k_hbm, v_hbm, ld_ref, w_ref, og_hbm,
     out_ref, gin_ref,
-    q_ref, k_ref, v_ref, og_ref, halo_ref, kext, kc, grow, after, mix, wts, att, ag, acc, ckg, gst,
+    q_ref, k_ref, v_ref, og_ref, halo_ref, kext, kc, grow, after, mix, wts, att, ag, acc, ckg, gst, sq,
     bt, bt_p, tot, bt_all, acc_sq, acc_dot, tpbuf,
     s_m, s_t, s_out, s_in, p_out, p_in, p_half, p_stage,
     b_m, b_t, b_out, b_in, a_out, a_in, a_half, a_stage,
     here, load_sem, halo_s, halo_r, bp_s, bp_r, bt_s, bt_r, tp_s, tp_r,
     s_s, s_r, p_s, p_r, b_s, b_r, a_s, a_r,
-    sx_s, sx_r, px_s, px_r, bx_s, bx_r, ax_s, ax_r, ch_s, ch_r, pp_s, pp_r,
+    sx_s, sx_r, px_s, px_r, bx_s, bx_r, ax_s, ax_r, ch_s, ch_r, pp_s, pp_r, pl_s, pl_r,
 ):
     toks, feats = q_hbm.shape
     heads = ld_ref.shape[0]
@@ -379,6 +380,7 @@
             w = (scores * mix[h]).astype(BF16)
             wts[h] = w
             att[:, hs] = dot(w, v_ref[:, hs], NN)
+            sq[:, hs] = (q_ref[:, hs].astype(F32) * grow[:, hs]).astype(BF16)
         return 0
 
     lax.fori_loop(0, steps, inside, 0)
@@ -431,11 +433,9 @@
             h = own_last(g * group + j)
             hs = lanes(h)
             normed = att[:, hs] * inv
-            out_ref[:, hs] = normed.astype(BF16)
             grad = ((og_ref[:, hs].astype(F32) - normed * shift) * inv).astype(BF16)
             ag[:, hs] = grad
-            sq = (q_ref[:, hs].astype(F32) * grow[:, hs]).astype(BF16)
-            b_m[h] = dot(sq, grad, TN)
+            b_m[h] = dot(sq[:, hs], grad, TN)
 
         @pl.when(g < half_steps)
         def _():
@@ -452,6 +452,7 @@
             h = g * group + j
             hs = lanes(h)
             grad = ag[:, hs]
+            out_ref[:, hs] = (att[:, hs] * inv).astype(BF16)
             sg = (dot(grad, v_ref[:, hs], NT) * mix[h]).astype(BF16)
             qg = dot(sg, kc[:, hs], NN) + grow[:, hs] * dot(grad, p_half[h], NT)
             acc[:, hs] = qg + dot(wts[h], grad, TN)
@@ -468,6 +469,27 @@
             ckg.at[pl.ds(0, HALO), hs], ckg.at[pl.ds(toks, HALO), hs], ch_s.at[h], ch_r.at[h],
             {"ctx": lax.rem(ctx + ctx_n - 1, ctx_n)},
         )
+
+    most = toks - LAST
+
+    def summed(h, first, size):
+        hs = lanes(h)
+        total = acc[pl.ds(first, size), hs]
+        for tap in range(taps):
+            total = total + w_ref[pl.ds(tap, 1), hs] * ckg[pl.ds(first + tap, size), hs]
+        gst[pl.ds(first, size), hs] = total.astype(BF16)
+
+    def back(h):
+        piece = (pl.ds(0, most), lanes(h))
+        return remote(
+            gst.at[piece], gin_ref.at[piece], pp_s.at[h], pp_r.at[h],
+            {"pp": lax.rem(pp + pp_n - 1, pp_n)},
+        )
+
+    back_last = remote(
+        gst.at[pl.ds(most, LAST), :], gin_ref.at[pl.ds(most, LAST), :], pl_s, pl_r,
+        {"pp": lax.rem(pp + pp_n - 1, pp_n)},
+    )
 
     def outside_grads(g, _):
         handed(a_stage, a_half, ax_s, ax_r, g)
@@ -484,39 +506,33 @@
             for j in range(group):
                 edge(own_first(g * group + j)).start()
 
+        for j in range(group):
+            summed(own_first(g * group + j), 0, most)
+
+        @pl.when(pp > 0)
+        def _():
+            for j in range(group):
+                back(own_first(g * group + j)).start()
+
         return 0
 
     lax.fori_loop(0, steps, outside_grads, 0)
-
-    def back(h):
-        hs = lanes(h)
-        return remote(
-            gst.at[:, hs], gin_ref.at[:, hs], pp_s.at[h], pp_r.at[h],
-            {"pp": lax.rem(pp + pp_n - 1, pp_n)},
-        )
 
     def finish(g, _):
         @pl.when(ctx < ctx_n - 1)
         def _():
             for j in range(group):
-                edge(own_first(g * group + j)).wait_recv()
+                edge(own_last(g * group + j)).wait_recv()
 
         for j in range(group):
-            h = own_first(g * group + j)
-            hs = lanes(h)
-            total = acc[:, hs]
-            for tap in range(taps):
-                total = total + w_ref[pl.ds(tap, 1), hs] * ckg[pl.ds(tap, toks), hs]
-            gst[:, hs] = total.astype(BF16)
-
-        @pl.when(pp > 0)
-        def _():
-            for j in range(group):
-                back(own_first(g * group + j)).start()
-
+            summed(own_last(g * group + j), most, LAST)
         return 0
 
     lax.fori_loop(0, steps, finish, 0)
+
+    @pl.when(pp > 0)
+    def _():
+        back_last.start()
 
     @pl.when(ctx < ctx_n - 1)
     def _():
@@ -575,6 +591,7 @@
             return 0
 
         lax.fori_loop(0, heads, leave, 0)
+        back_last.wait_send()
 
     @pl.when(pp < pp_n - 1)
     def _():
@@ -583,6 +600,27 @@
             return 0
 
         lax.fori_loop(0, heads, land, 0)
+        back_last.wait_recv()
+
+
+def place(a_ref, b_ref, c_ref, d_ref, buf, sem_in, sem_out):
+    step = a_ref.shape[0] // 4
+    pieces = []
+    for n, (src, dst) in enumerate(((a_ref, c_ref), (b_ref, d_ref))):
+        for p in range(4):
+            rows = pl.ds(p * step, step)
+            held = buf.at[n, rows]
+            pieces.append((
+                pltpu.make_async_copy(src.at[rows], held, sem_in.at[n, p]),
+                pltpu.make_async_copy(held, dst.at[rows], sem_out.at[n, p]),
+            ))
+    for get, _ in pieces:
+        get.start()
+    for get, put in pieces:
+        get.wait()
+        put.start()
+    for _, put in pieces:
+        put.wait()
 
 
 def solution(mesh):
@@ -611,7 +649,7 @@
         scratch = [
             flat_b, flat_b, flat_b, flat_b, pltpu.VMEM((16, feats), BF16), longer, flat_b,
             flat_f, flat_f, pltpu.VMEM((heads, toks, toks), F32),
-            pltpu.VMEM((heads, toks, toks), BF16), flat_f, flat_b, flat_f, longer, flat_b,
+            pltpu.VMEM((heads, toks, toks), BF16), flat_f, flat_b, flat_f, longer, flat_b, flat_b,
             totals, totals, pltpu.VMEM((half, 1, hd), F32), pltpu.VMEM((chips, 1, hd), F32),
             square, square,
             pltpu.VMEM((tp_n, 8, toks), F32),
@@ -620,7 +658,7 @@
         scratch += [pltpu.SemaphoreType.REGULAR((chips,))]
         scratch += [dma((4,)), dma, dma, dma, dma, dma((chips,)), dma((chips,))]
         scratch += [dma((max(tp_n - 1, 1),))] * 2 + [dma((chips,))] * 8 + [dma((half,))] * 8
-        scratch += [dma((heads,))] * 4
+        scratch += [dma((heads,))] * 4 + [dma, dma]
         whole = pl.BlockSpec(memory_space=pltpu.VMEM)
         there = pl.BlockSpec(memory_space=pl.ANY)
 
@@ -640,6 +678,15 @@
         )(
             queries[0], key_input[0], values[0], log_decay[0].T, conv_weight[0], out_grad[0]
         )
+        out, gin = pl.pallas_call(
+            place,
+            out_shape=(shape, shape),
+            in_specs=[there, there],
+            out_specs=(there, there),
+            scratch_shapes=[
+                pltpu.VMEM((2, toks, feats), BF16), dma((2, 4)), dma((2, 4)),
+            ],
+        )(out, gin)
         return out[None], gin[None]
 
     placed = (

time: 74.8 us -> 71.5 us (0.956)
  local copies, waits for them, and re-layouts: 2.42 us -> 0 us
  Pallas kernels: 71.5 us -> 70.2 us
    pallas_call x1, Pallas kernels: 71.5 us -> 68.4 us  [per_device(): pl.pallas_call(body, out_shape=(shape, shape), in_specs=[there, there, th...]
    unnamed x4 -> x0, local copies, waits for them, and re-layouts: 2.42 us -> none
    pallas_call x0 -> x1, Pallas kernels: none -> 1.83 us  [per_device(): pl.pallas_call(place, out_shape=(shape, shape), in_specs=[there, there],...]
where the time goes in v5:
time: 71.5 us; the launch traced here: 70.9 us
  Pallas kernels  70.2 us (98%)
    pallas_call x1, Pallas kernels, per_device(): pl.pallas_call(body, out_shape=(shape, shape), in_specs=[there, there, th...  68.4 us
    pallas_call x1, Pallas kernels, per_device(): pl.pallas_call(place, out_shape=(shape, shape), in_specs=[there, there],...  1.83 us

profile of v5, /device:TPU:25, one launch (start us, length us, event | category | flops | bytes accessed | tf_op | source)
XLA Modules:
  0.0 70.9 jit_solution(14179230300754402887)
XLA Ops:
  0.6 68.4 %shard_map.77 = (bf16[128,1024]{1,0:T(8,128)(2,1)}, bf16[128,1024]{1,0:T(8,128)(2,1)}) custom-call(bf16[128,1024]{1,0:T(8,128)(2,1)} %bitcast.10, bf16[128,1024]{1,0:T(8,128)(2,1)} %bitcast.11, bf16[128,1024]{1,0:T(8,128)(2,1)} %bitcast.12, f32[8,128]{1,0:T(8,128)} %bitcast.15, f32[4,1024]{1,0:T(4,128)} %bitcast.14, bf16[128,1024]{1,0:T(8,128)(2,1)} %bitcast.13), custom_call_target="tpu_custom_call" | custom-call | tf_op jit(solution)/shard_map/pallas_call | solution.py:669
  69.0 1.8 %shard_map.78 = (bf16[128,1024]{1,0:T(8,128)(2,1)}, bf16[128,1024]{1,0:T(8,128)(2,1)}) custom-call(bf16[128,1024]{1,0:T(8,128)(2,1)} %get-tuple-element.6.a_ref, bf16[128,1024]{1,0:T(8,128)(2,1)} %get-tuple-element.7.b_ref), custom_call_target="tpu_custom_call" | custom-call | tf_op jit(solution)/shard_map/pallas_call | solution.py:681

commit v6 on v5

--- a/solution.py
+++ b/solution.py
@@ -35,9 +35,9 @@
 
 def kernel(
     ctx_n, tp_n, pp_n,
-    q_hbm, k_hbm, v_hbm, ld_ref, w_ref, og_hbm,
+    q_hbm, k_hbm, v_hbm, ld_hbm, w_hbm, og_hbm,
     out_ref, gin_ref,
-    q_ref, k_ref, v_ref, og_ref, halo_ref, kext, kc, grow, after, mix, wts, att, ag, acc, ckg, gst, sq,
+    ld_ref, w_ref, q_ref, k_ref, v_ref, og_ref, halo_ref, kext, kc, grow, after, mix, wts, att, ag, acc, ckg, gst, sq,
     bt, bt_p, tot, bt_all, acc_sq, acc_dot, tpbuf,
     s_m, s_t, s_out, s_in, p_out, p_in, p_half, p_stage,
     b_m, b_t, b_out, b_in, a_out, a_in, a_half, a_stage,
@@ -46,9 +46,9 @@
     sx_s, sx_r, px_s, px_r, bx_s, bx_r, ax_s, ax_r, ch_s, ch_r, pp_s, pp_r, pl_s, pl_r,
 ):
     toks, feats = q_hbm.shape
-    heads = ld_ref.shape[0]
+    heads = ld_hbm.shape[0]
     hd = feats // heads
-    taps = w_ref.shape[0]
+    taps = w_hbm.shape[0]
     width_all = feats * tp_n
     parts = ctx_n // heads
     rows = s_in.shape[1]
@@ -105,11 +105,14 @@
     loads = [
         pltpu.make_async_copy(src, dst, load_sem.at[n])
         for n, (src, dst) in enumerate(
-            ((k_hbm, k_ref), (v_hbm, v_ref), (q_hbm, q_ref), (og_hbm, og_ref))
+            (
+                (k_hbm, k_ref), (v_hbm, v_ref), (q_hbm, q_ref), (og_hbm, og_ref),
+                (ld_hbm, ld_ref), (w_hbm, w_ref),
+            )
         )
     ]
-    for load in loads:
-        load.start()
+    for n in (4, 0, 5, 1, 2, 3):
+        loads[n].start()
 
     pl.semaphore_wait(barrier, len(greet) + 2 * chip + (pp + pp_n - 1) // pp_n)
 
@@ -123,6 +126,7 @@
     cols_i = lax.broadcasted_iota(jnp.int32, (toks, toks), 1)
     causal = rows_i >= cols_i
     tri = causal.astype(F32)
+    loads[4].wait()
     ld = ld_ref[...]
     cd = lax.dot_general(
         tri, ld, (NT, ((), ())), precision=lax.Precision.HIGHEST, preferred_element_type=F32
@@ -171,6 +175,7 @@
         gin_ref[...] = jnp.zeros_like(gin_ref)
 
     loads[0].wait()
+    loads[5].wait()
     kext[pl.ds(HALO, toks), :] = k_ref[...].astype(F32)
     loads[1].wait()
 
@@ -603,23 +608,14 @@
         back_last.wait_recv()
 
 
-def place(a_ref, b_ref, c_ref, d_ref, buf, sem_in, sem_out):
-    step = a_ref.shape[0] // 4
-    pieces = []
-    for n, (src, dst) in enumerate(((a_ref, c_ref), (b_ref, d_ref))):
-        for p in range(4):
-            rows = pl.ds(p * step, step)
-            held = buf.at[n, rows]
-            pieces.append((
-                pltpu.make_async_copy(src.at[rows], held, sem_in.at[n, p]),
-                pltpu.make_async_copy(held, dst.at[rows], sem_out.at[n, p]),
-            ))
-    for get, _ in pieces:
-        get.start()
-    for get, put in pieces:
-        get.wait()
+def place(a_ref, b_ref, c_ref, d_ref, sems):
+    puts = [
+        pltpu.make_async_copy(src, dst, sems.at[n])
+        for n, (src, dst) in enumerate(((a_ref, c_ref), (b_ref, d_ref)))
+    ]
+    for put in puts:
         put.start()
-    for _, put in pieces:
+    for put in puts:
         put.wait()
 
 
@@ -647,6 +643,7 @@
         longer = pltpu.VMEM((toks + HALO, feats), F32)
         square = pltpu.VMEM((toks, hd), F32)
         scratch = [
+            pltpu.VMEM((heads, toks), F32), pltpu.VMEM((conv_weight.shape[1], feats), F32),
             flat_b, flat_b, flat_b, flat_b, pltpu.VMEM((16, feats), BF16), longer, flat_b,
             flat_f, flat_f, pltpu.VMEM((heads, toks, toks), F32),
             pltpu.VMEM((heads, toks, toks), BF16), flat_f, flat_b, flat_f, longer, flat_b, flat_b,
@@ -656,12 +653,15 @@
         ]
         scratch += scanned + scanned
         scratch += [pltpu.SemaphoreType.REGULAR((chips,))]
-        scratch += [dma((4,)), dma, dma, dma, dma, dma((chips,)), dma((chips,))]
+        scratch += [dma((6,)), dma, dma, dma, dma, dma((chips,)), dma((chips,))]
         scratch += [dma((max(tp_n - 1, 1),))] * 2 + [dma((chips,))] * 8 + [dma((half,))] * 8
         scratch += [dma((heads,))] * 4 + [dma, dma]
         whole = pl.BlockSpec(memory_space=pltpu.VMEM)
         there = pl.BlockSpec(memory_space=pl.ANY)
 
+        def stay(x):
+            return pltpu.with_memory_space_constraint(x, pltpu.HBM)
+
         def body(*refs):
             kernel(ctx_n, tp_n, pp_n, *refs)
 
@@ -669,23 +669,23 @@
         out, gin = pl.pallas_call(
             body,
             out_shape=(shape, shape),
-            in_specs=[there, there, there, whole, whole, there],
+            in_specs=[there] * 6,
             out_specs=(whole, whole),
             scratch_shapes=scratch,
             compiler_params=pltpu.CompilerParams(
-                collective_id=0, has_side_effects=True, vmem_limit_bytes=63 * 1024 * 1024
+                collective_id=0, has_side_effects=True, vmem_limit_bytes=40 * 1024 * 1024
             ),
         )(
-            queries[0], key_input[0], values[0], log_decay[0].T, conv_weight[0], out_grad[0]
+            stay(queries[0]), stay(key_input[0]), stay(values[0]), stay(log_decay[0].T),
+            stay(conv_weight[0]), stay(out_grad[0]),
         )
         out, gin = pl.pallas_call(
             place,
             out_shape=(shape, shape),
-            in_specs=[there, there],
+            in_specs=[whole, whole],
             out_specs=(there, there),
-            scratch_shapes=[
-                pltpu.VMEM((2, toks, feats), BF16), dma((2, 4)), dma((2, 4)),
-            ],
+            scratch_shapes=[dma((2,))],
+            compiler_params=pltpu.CompilerParams(vmem_limit_bytes=1024 * 1024),
         )(out, gin)
         return out[None], gin[None]
 

time: 71.5 us -> 69 us (0.965)
  Pallas kernels: 70.2 us -> 67.9 us
    pallas_call x2, Pallas kernels: 70.2 us -> 67.9 us  [the longest x1 67.1 us: per_device(): pl.pallas_call(body, out_shape=(shape, shape), in_specs=[there] * 6, out_...]
where the time goes in v6:
time: 69 us; the launch traced here: 68.5 us
  Pallas kernels  67.9 us (98%)
    pallas_call x1, Pallas kernels, per_device(): pl.pallas_call(body, out_shape=(shape, shape), in_specs=[there] * 6, out_...  67.1 us

profile of v6, /device:TPU:25, one launch (start us, length us, event | category | flops | bytes accessed | tf_op | source)
XLA Modules:
  0.0 68.5 jit_solution(2016456694252336571)
XLA Ops:
  0.6 67.1 %shard_map.77 = (bf16[128,1024]{1,0:T(8,128)(2,1)S(1)}, bf16[128,1024]{1,0:T(8,128)(2,1)S(1)}) custom-call(bf16[128,1024]{1,0:T(8,128)(2,1)} %bitcast.10, bf16[128,1024]{1,0:T(8,128)(2,1)} %bitcast.11, bf16[128,1024]{1,0:T(8,128)(2,1)} %bitcast.12, f32[8,128]{1,0:T(8,128)} %bitcast.15, f32[4,1024]{1,0:T(4,128)} %bitcast.14, bf16[128,1024]{1,0:T(8,128)(2,1)} %bitcast.13), custom_call_target="tpu_custom_call" | custom-call | tf_op jit(solution)/shard_map/pallas_call | solution.py:669
  67.7 0.8 %shard_map.78 = (bf16[128,1024]{1,0:T(8,128)(2,1)}, bf16[128,1024]{1,0:T(8,128)(2,1)}) custom-call(bf16[128,1024]{1,0:T(8,128)(2,1)S(1)} %get-tuple-element.6.a_ref, bf16[128,1024]{1,0:T(8,128)(2,1)S(1)} %get-tuple-element.7.b_ref), custom_call_target="tpu_custom_call" | custom-call | tf_op jit(solution)/shard_map/pallas_call | solution.py:682

commit v7 on v6

--- a/solution.py
+++ b/solution.py
@@ -261,9 +261,6 @@
                     def _():
                         spread(out, into, send_sem, recv_sem, i, part).start()
 
-                    if opening:
-                        total_to(i, part).start()
-
                 @pl.when(h * parts + part == ctx)
                 def _():
                     size = rows if part < parts - 1 else short
@@ -274,16 +271,29 @@
 
         lax.fori_loop(0, half, one, 0)
 
+        def tell(i, _):
+            for part in range(parts):
+                @pl.when((own0 + i) * parts + part != ctx)
+                def _():
+                    total_to(i, part).start()
+
+            return 0
+
+        if opening:
+            lax.fori_loop(0, half, tell, 0)
+
     def scan(into, recv_sem, out, home, send_sem, home_sem, opening):
         def give(z, carry):
             out[z] = carry.astype(BF16)
-            if opening:
-                late = jnp.where(z >= chips // 2, 1, 0)
-
-                @pl.when(late != core)
-                def _():
-                    meet(z)
-
+            late = jnp.where(z >= chips // 2, 1, 0)
+
+            @pl.when(late != core)
+            def _():
+                meet(z)
+
+            send(z)
+
+        def send(z):
             @pl.when(2 * z + scan_core != ctx)
             def _():
                 sized(lambda size: deliver(out, home, send_sem, home_sem, z, size).start())
@@ -302,11 +312,31 @@
         if not opening:
             total_in(chips - 1)
 
+            def ready(z, _):
+                @pl.when(2 * z + scan_core != ctx)
+                def _():
+                    sized(lambda size: arrive(into, recv_sem, z, size).wait_recv())
+
+                return 0
+
+            lax.fori_loop(1, chips, ready, 0)
+            carry = jnp.zeros((rows, hd), F32)
+            for z in range(chips - 1, -1, -1):
+                out[z] = carry.astype(BF16)
+                if z > 0:
+                    carry = jnp.exp(bt_all[z]) * carry + into[z].astype(F32)
+
+            def serve(z, _):
+                send(z)
+                return 0
+
+            lax.fori_loop(0, chips, serve, 0)
+            return
+
         def one(n, carry):
-            z = n if opening else chips - 1 - n
+            z = n
             give(z, carry)
-            if opening:
-                total_in(z)
+            total_in(z)
 
             @pl.when(2 * z + scan_core != ctx)
             def _():
@@ -315,7 +345,7 @@
             return jnp.exp(bt_all[z]) * carry + into[z].astype(F32)
 
         carry = lax.fori_loop(0, chips - 1, one, jnp.zeros((rows, hd), F32))
-        give(chips - 1 if opening else 0, carry)
+        give(chips - 1, carry)
 
     def hand(stage, dest, send_sem, recv_sem, i, h):
         return remote(

time: 69 us -> 67.8 us (0.983)
  Pallas kernels: 67.9 us -> 67 us
    pallas_call x1, Pallas kernels: 67.1 us -> 66.2 us  [per_device(): pl.pallas_call(body, out_shape=(shape, shape), in_specs=[there] * 6, out_...]
where the time goes in v7:
time: 67.8 us; the launch traced here: 67.6 us
  Pallas kernels  67 us (99%)
    pallas_call x1, Pallas kernels, per_device(): pl.pallas_call(body, out_shape=(shape, shape), in_specs=[there] * 6, out_...  66.2 us

profile of v7, /device:TPU:25, one launch (start us, length us, event | category | flops | bytes accessed | tf_op | source)
XLA Modules:
  0.0 67.6 jit_solution(10101294227849453726)
XLA Ops:
  0.6 66.2 %shard_map.77 = (bf16[128,1024]{1,0:T(8,128)(2,1)S(1)}, bf16[128,1024]{1,0:T(8,128)(2,1)S(1)}) custom-call(bf16[128,1024]{1,0:T(8,128)(2,1)} %bitcast.10, bf16[128,1024]{1,0:T(8,128)(2,1)} %bitcast.11, bf16[128,1024]{1,0:T(8,128)(2,1)} %bitcast.12, f32[8,128]{1,0:T(8,128)} %bitcast.15, f32[4,1024]{1,0:T(4,128)} %bitcast.14, bf16[128,1024]{1,0:T(8,128)(2,1)} %bitcast.13), custom_call_target="tpu_custom_call" | custom-call | tf_op jit(solution)/shard_map/pallas_call | solution.py:699
  66.8 0.8 %shard_map.78 = (bf16[128,1024]{1,0:T(8,128)(2,1)}, bf16[128,1024]{1,0:T(8,128)(2,1)}) custom-call(bf16[128,1024]{1,0:T(8,128)(2,1)S(1)} %get-tuple-element.6.a_ref, bf16[128,1024]{1,0:T(8,128)(2,1)S(1)} %get-tuple-element.7.b_ref), custom_call_target="tpu_custom_call" | custom-call | tf_op jit(solution)/shard_map/pallas_call | solution.py:712

commit v8 on v7

--- a/solution.py
+++ b/solution.py
@@ -82,26 +82,6 @@
     barrier = pltpu.get_barrier_semaphore()
     greet = [{"ctx": partner}]
     greet += [{"tp": lax.rem(tp + step, tp_n)} for step in range(1, tp_n)]
-    for where in greet:
-        pl.semaphore_signal(barrier, inc=1, device_id=where, device_id_type=MESH)
-
-    @pl.when(pp < pp_n - 1)
-    def _():
-        pl.semaphore_signal(
-            barrier, inc=1, device_id={"pp": lax.rem(pp + 1, pp_n)}, device_id_type=MESH
-        )
-
-    def enter(peer, _):
-        pl.semaphore_signal(barrier, inc=1, device_id={"ctx": peer}, device_id_type=MESH)
-        return 0
-
-    lax.fori_loop(2 * chip + 2, ctx_n, enter, 0)
-
-    def meet(z):
-        @pl.when(jnp.logical_and(z > chip, z != chip + core))
-        def _():
-            pl.semaphore_wait(here.at[z], 2)
-
     loads = [
         pltpu.make_async_copy(src, dst, load_sem.at[n])
         for n, (src, dst) in enumerate(
@@ -111,13 +91,36 @@
             )
         )
     ]
-    for n in (4, 0, 5, 1, 2, 3):
+    loads[4].start()
+    loads[0].start()
+    for where in greet:
+        pl.semaphore_signal(barrier, inc=1, device_id=where, device_id_type=MESH)
+
+    @pl.when(pp < pp_n - 1)
+    def _():
+        pl.semaphore_signal(
+            barrier, inc=1, device_id={"pp": lax.rem(pp + 1, pp_n)}, device_id_type=MESH
+        )
+
+    def enter(peer, _):
+        pl.semaphore_signal(barrier, inc=1, device_id={"ctx": peer}, device_id_type=MESH)
+        return 0
+
+    lax.fori_loop(2 * chip + 2, ctx_n, enter, 0)
+
+    def meet(z):
+        @pl.when(jnp.logical_and(z > chip, z != chip + core))
+        def _():
+            pl.semaphore_wait(here.at[z], 2)
+
+    for n in (5, 1, 2, 3):
         loads[n].start()
 
     pl.semaphore_wait(barrier, len(greet) + 2 * chip + (pp + pp_n - 1) // pp_n)
 
     def answer(peer, _):
-        pl.semaphore_signal(here.at[chip], inc=1, device_id={"ctx": peer}, device_id_type=MESH)
+        near = 2 * chip - 1 - peer
+        pl.semaphore_signal(here.at[chip], inc=1, device_id={"ctx": near}, device_id_type=MESH)
         return 0
 
     lax.fori_loop(0, 2 * chip, answer, 0)

time: 67.8 us -> 66.7 us (0.984)
  Pallas kernels: 67 us -> 65.9 us
    pallas_call x1, Pallas kernels: 66.2 us -> 65.1 us  [per_device(): pl.pallas_call(body, out_shape=(shape, shape), in_specs=[there] * 6, out_...]
where the time goes in v8:
time: 66.7 us; the launch traced here: 66.5 us
  Pallas kernels  65.9 us (99%)
    pallas_call x1, Pallas kernels, per_device(): pl.pallas_call(body, out_shape=(shape, shape), in_specs=[there] * 6, out_...  65.1 us

profile of v8, /device:TPU:25, one launch (start us, length us, event | category | flops | bytes accessed | tf_op | source)
XLA Modules:
  0.0 66.5 jit_solution(11978816058123329495)
XLA Ops:
  0.6 65.1 %shard_map.77 = (bf16[128,1024]{1,0:T(8,128)(2,1)S(1)}, bf16[128,1024]{1,0:T(8,128)(2,1)S(1)}) custom-call(bf16[128,1024]{1,0:T(8,128)(2,1)} %bitcast.10, bf16[128,1024]{1,0:T(8,128)(2,1)} %bitcast.11, bf16[128,1024]{1,0:T(8,128)(2,1)} %bitcast.12, f32[8,128]{1,0:T(8,128)} %bitcast.15, f32[4,1024]{1,0:T(4,128)} %bitcast.14, bf16[128,1024]{1,0:T(8,128)(2,1)} %bitcast.13), custom_call_target="tpu_custom_call" | custom-call | tf_op jit(solution)/shard_map/pallas_call | solution.py:702
  65.7 0.8 %shard_map.78 = (bf16[128,1024]{1,0:T(8,128)(2,1)}, bf16[128,1024]{1,0:T(8,128)(2,1)}) custom-call(bf16[128,1024]{1,0:T(8,128)(2,1)S(1)} %get-tuple-element.6.a_ref, bf16[128,1024]{1,0:T(8,128)(2,1)S(1)} %get-tuple-element.7.b_ref), custom_call_target="tpu_custom_call" | custom-call | tf_op jit(solution)/shard_map/pallas_call | solution.py:715
